TPU v7x, 32 devices: a whole 2x2x4 slice. The times are simulated.
32 devices in a mesh: req: 4 (over z), mlp: 8 (over y, x, core).
Axes of the slice: x: 2, y: 2, z: 4, core: 2. Of those that a mesh axis runs over, the one named last changes fastest.
Arguments:
- tokens: bfloat16 [1024, 5120], P(('req', 'mlp')), may hold values from -6 to 6
- modulation: float32 [16, 6, 5120], P('req'), may hold values from -3 to 3
- lengths: int32 [4, 4], P('req'), may hold values from 1 to 160, 256 in all within a row
- request_adapter: int32 [16], P('req'), may hold values from 0 to 31
- adapter_storage: int32 [32], replicated, may hold values from 0 to 31, each once
- adapter_down_weight: bfloat16 [32, 5120, 32], P('mlp'), may hold values from -0.078125 to 0.078125
- adapter_up_maps: bfloat16 [32, 2, 16, 4096], P('mlp'), may hold values from -1.5 to 1.5
- input_projection: bfloat16 [4, 5120, 4096], P(None, None, 'mlp'), may hold values from -0.078125 to 0.078125
- query_key_gains: float32 [3, 4096], P(None, 'mlp'), may hold values from 0.1 to 1.9
- positions: int32 [3, 1024], P(None, 'req'), may hold values from 0 to 63
- block_page_lookup: int32 [4, 16], P('req'), may hold values from 0 to 15, each once within a row
- output_projection: bfloat16 [2, 4096, 5120], P(None, 'mlp'), may hold values from -0.09375 to 0.09375
- cross_norm_gain: float32 [5120], replicated, may hold values from 0.1 to 1.9
- text_token_cache: bfloat16 [2, 16, 512, 4096], P(None, 'req', None, 'mlp'), may hold values from -3 to 3
- feedforward_up: bfloat16 [5120, 8192], P('req', 'mlp'), may hold values from -0.078125 to 0.078125
- feedforward_down: bfloat16 [8192, 5120], P('mlp', 'req'), may hold values from -0.0625 to 0.0625
Outputs:
- layer_out: bfloat16 [1024, 5120], P(('req', 'mlp'))
- kv_pages: bfloat16 [2, 64, 16, 4096], P(None, 'req', None, 'mlp')
Inputs may be any that keep to these rules, and one draw needn't show every extreme that they name: `lengths`: row g lists the token counts of the 4 requests of group g in order; they fill the group's 256 positions, and the largest is 160. A permutation: adapter a is stored at index adapter_storage[a] of adapter_down_weight and adapter_up_maps. `block_page_lookup`: each row is a permutation of a group's 16 pages.
All inputs are finite; a program needn't handle non-finite values.
Results may differ from a plain program's by a relative error of at most 0.017.
Values may be sent and summed in bfloat16 or wider, within the bound.
A program may use at most 192 MiB of HBM per device.

v0:
```python
import math

import jax
import jax.numpy as jnp
from jax import lax
from jax.sharding import PartitionSpec as P

HD = 128
PAGE = 16


EPSILON = 1e-06


def as_sent(array):

    def short(part):
        return part.astype(jnp.bfloat16) if part.dtype == jnp.float32 else part

    return jax.tree.map(short, array)


def layer_norm(values):
    center = values - jnp.mean(values, axis=-1, keepdims=True)
    spread = jnp.mean(center * center, axis=-1, keepdims=True)
    return center * lax.rsqrt(spread + EPSILON)


def rotary_tables(grid):
    half_dim = HD // 2
    spatial = half_dim // 3
    temporal = half_dim - 2 * spatial
    column = jnp.arange(half_dim, dtype=jnp.int32)
    which_axis = jnp.where(
        column < temporal, 0, jnp.where(column < temporal + spatial, 1, 2)
    ).astype(jnp.int32)
    offset = jnp.where(
        which_axis == 0, 0, jnp.where(which_axis == 1, temporal, temporal + spatial)
    ).astype(jnp.int32)
    span_size = jnp.where(which_axis == 0, temporal, spatial).astype(jnp.float32)
    frequency = jnp.exp(-(column - offset).astype(jnp.float32) / span_size * math.log(10000.0))
    coordinate = grid.astype(jnp.float32)[which_axis, :].T
    angles = coordinate * frequency[None, :]
    return (jnp.cos(angles), jnp.sin(angles))


def rotate(values, cosine, sine_part):
    half_dim = HD // 2
    front_half = values[..., :half_dim]
    back_half = values[..., half_dim:]
    cosine = cosine[:, None, :]
    sine_part = sine_part[:, None, :]
    return jnp.concatenate(
        [front_half * cosine - back_half * sine_part, back_half * cosine + front_half * sine_part],
        axis=-1,
    )


def attend(queries, key_rows, value_rows, allowed):
    scores = jnp.einsum(
        "thd,shd->hts", queries, key_rows, preferred_element_type=jnp.float32
    ) / math.sqrt(HD)
    scores = jnp.where(allowed[None], scores, -1e30)
    weights = jnp.exp(scores)
    weights = (weights / jnp.sum(weights, axis=-1, keepdims=True)).astype(jnp.bfloat16)
    return jnp.einsum(
        "hts,shd->thd", weights, value_rows, preferred_element_type=jnp.float32
    ).astype(jnp.bfloat16)


def choose_rows(table, segment):
    chosen = jnp.zeros((segment.shape[0],) + table.shape[1:], table.dtype)
    for request in range(table.shape[0]):
        picked = (segment == request).reshape((-1,) + (1,) * (table.ndim - 1))
        chosen = jnp.where(picked, table[request][None], chosen)
    return chosen


def body(
    tokens,
    modulation,
    lengths,
    request_adapter,
    adapter_storage,
    adapter_down_weight,
    adapter_up_maps,
    input_projection,
    query_key_gains,
    positions,
    block_page_lookup,
    output_projection,
    cross_norm_gain,
    text_token_cache,
    feedforward_up,
    feedforward_down,
):
    mlp_count = lax.axis_size("mlp")
    my_index = lax.axis_index("mlp")
    own_count = tokens.shape[0]
    group_rows = own_count * mlp_count
    local_width = input_projection.shape[2]
    heads_local = local_width // HD
    entire_width = local_width * mlp_count
    resident_slots = adapter_down_weight.shape[0]
    doubled_rank = adapter_down_weight.shape[2]
    rank_once = doubled_rank // 2

    def over_group(own_rows, row_fn):
        return row_fn(lax.all_gather(own_rows, "mlp", axis=0, tiled=True), jnp.int32(0))

    def sum_rows(term_fn):
        return lax.psum_scatter(
            term_fn(jnp.int32(0), own_count * lax.axis_size("mlp")).astype(jnp.bfloat16),
            "mlp",
            scatter_dimension=0,
            tiled=True,
        ).astype(jnp.float32)

    def global_sum(pieces):
        return jax.tree.map(lambda part: part.astype(jnp.float32), lax.psum(as_sent(pieces), "mlp"))

    up_full, down_full = (
        lax.all_gather(feedforward_up, "req", axis=0, tiled=True),
        lax.all_gather(feedforward_down, "req", axis=1, tiled=True),
    )
    adapter_up_weight = lax.all_to_all(
        adapter_up_maps, "mlp", split_axis=3, concat_axis=0, tiled=True
    )
    slot_total = adapter_up_weight.shape[0]
    bounds = jnp.cumsum(lengths[0])
    position = jnp.arange(group_rows, dtype=jnp.int32)
    segment = jnp.sum((position[:, None] >= bounds[None, :]).astype(jnp.int32), axis=1)
    own_start = my_index * own_count
    own_segment = lax.dynamic_slice_in_dim(segment, own_start, own_count)
    per_token = [choose_rows(modulation[:, which_row, :], own_segment) for which_row in range(6)]
    token_f32 = tokens.astype(jnp.float32)
    normed_in = (layer_norm(token_f32) * (1.0 + per_token[1]) + per_token[0]).astype(jnp.bfloat16)

    def project_rows(incoming_rows, row_start):
        row_total = incoming_rows.shape[0]
        parts = [
            jnp.dot(incoming_rows, input_projection[which_map], preferred_element_type=jnp.float32)
            for which_map in range(3)
        ]
        code_block = jnp.einsum(
            "lf,sfe->lse", incoming_rows, adapter_down_weight, preferred_element_type=jnp.float32
        )
        parts.append(code_block.reshape(row_total, resident_slots * doubled_rank))
        return jnp.concatenate(parts, axis=1)

    projected = over_group(normed_in, project_rows)
    query_base = projected[:, :local_width]
    key_linear = projected[:, local_width : 2 * local_width]
    value_base = projected[:, 2 * local_width : 3 * local_width]
    code_block = projected[:, 3 * local_width :].reshape(group_rows, resident_slots, doubled_rank)
    request_slot = adapter_storage[request_adapter]
    token_slot = choose_rows(request_slot, segment)
    held = (
        token_slot[:, None]
        == my_index * resident_slots + jnp.arange(resident_slots, dtype=jnp.int32)[None, :]
    ).astype(jnp.float32)
    my_codes = jnp.sum(held[:, :, None] * code_block, axis=1)
    codes = global_sum(my_codes).astype(jnp.bfloat16)
    everywhere = (token_slot[:, None] == jnp.arange(slot_total, dtype=jnp.int32)[None, :]).astype(
        jnp.float32
    )

    def spread(code_part):
        return (
            (everywhere[:, :, None] * code_part[:, None, :].astype(jnp.float32))
            .reshape(group_rows, slot_total * rank_once)
            .astype(jnp.bfloat16)
        )

    query_up_weight = adapter_up_weight[:, 0].reshape(slot_total * rank_once, local_width)
    value_up_weight = adapter_up_weight[:, 1].reshape(slot_total * rank_once, local_width)
    query_linear = query_base + jnp.dot(
        spread(codes[:, :rank_once]), query_up_weight, preferred_element_type=jnp.float32
    )
    value_rows = (
        value_base
        + jnp.dot(spread(codes[:, rank_once:]), value_up_weight, preferred_element_type=jnp.float32)
    ).astype(jnp.bfloat16)
    query_square, key_square = global_sum(
        (jnp.sum(query_linear * query_linear, axis=1), jnp.sum(key_linear * key_linear, axis=1))
    )
    query_norm = (
        query_linear
        * lax.rsqrt(query_square / entire_width + EPSILON)[:, None]
        * query_key_gains[0]
    )
    key_norm = (
        key_linear * lax.rsqrt(key_square / entire_width + EPSILON)[:, None] * query_key_gains[1]
    )
    cosine, sine_part = rotary_tables(positions)
    query_rot = rotate(query_norm.reshape(group_rows, heads_local, HD), cosine, sine_part).astype(
        jnp.bfloat16
    )
    key_rot = rotate(key_norm.reshape(group_rows, heads_local, HD), cosine, sine_part).astype(
        jnp.bfloat16
    )
    value_heads = value_rows.reshape(group_rows, heads_local, HD)
    page_count = group_rows // PAGE
    stacked = jnp.stack(
        [
            key_rot.reshape(page_count, PAGE, local_width),
            value_rows.reshape(page_count, PAGE, local_width),
        ]
    )
    kv_pages = jnp.zeros_like(stacked).at[:, block_page_lookup[0]].set(stacked)
    allowed = segment[:, None] == segment[None, :]
    attended = attend(query_rot, key_rot, value_heads, allowed).reshape(group_rows, local_width)
    text_owner = (
        jnp.arange(text_token_cache.shape[1] * text_token_cache.shape[2], dtype=jnp.int32)
        // text_token_cache.shape[2]
    )
    cross_allowed = segment[:, None] == text_owner[None, :]
    text_keys = text_token_cache[0].reshape(-1, heads_local, HD)
    text_values = text_token_cache[1].reshape(-1, heads_local, HD)

    def attend_term(row_start, row_total):
        return jnp.dot(attended, output_projection[0], preferred_element_type=jnp.float32)

    first_res = (token_f32 + per_token[2] * sum_rows(attend_term)).astype(jnp.bfloat16)
    cross_own = (layer_norm(first_res.astype(jnp.float32)) * cross_norm_gain).astype(jnp.bfloat16)

    def cross_rows(incoming_rows, row_start):
        return jnp.dot(incoming_rows, input_projection[3], preferred_element_type=jnp.float32)

    cross_linear = over_group(cross_own, cross_rows)
    cross_square = global_sum(jnp.sum(cross_linear * cross_linear, axis=1))
    cross_query = (
        cross_linear
        * lax.rsqrt(cross_square / entire_width + EPSILON)[:, None]
        * query_key_gains[2]
    ).astype(jnp.bfloat16)
    cross_out = attend(
        cross_query.reshape(group_rows, heads_local, HD), text_keys, text_values, cross_allowed
    ).reshape(group_rows, local_width)

    def cross_term(row_start, row_total):
        return jnp.dot(cross_out, output_projection[1], preferred_element_type=jnp.float32)

    second_res = (first_res.astype(jnp.float32) + sum_rows(cross_term)).astype(jnp.bfloat16)
    mlp_own = (
        layer_norm(second_res.astype(jnp.float32)) * (1.0 + per_token[4]) + per_token[3]
    ).astype(jnp.bfloat16)

    def expand_rows(incoming_rows, row_start):
        return jax.nn.gelu(
            jnp.dot(incoming_rows, up_full, preferred_element_type=jnp.float32), approximate=True
        ).astype(jnp.bfloat16)

    hidden = over_group(mlp_own, expand_rows)

    def down_term(row_start, row_total):
        return jnp.dot(hidden, down_full, preferred_element_type=jnp.float32)

    layer_out = (second_res.astype(jnp.float32) + per_token[5] * sum_rows(down_term)).astype(
        jnp.bfloat16
    )
    return (layer_out, kv_pages)


def solution(mesh):
    return jax.shard_map(
        body,
        mesh=mesh,
        in_specs=(
            P(("req", "mlp"), None),
            P("req", None, None),
            P("req", None),
            P("req"),
            P(),
            P("mlp", None, None),
            P("mlp", None, None, None),
            P(None, None, "mlp"),
            P(None, "mlp"),
            P(None, "req"),
            P("req", None),
            P(None, "mlp", None),
            P(),
            P(None, "req", None, "mlp"),
            P("req", "mlp"),
            P("mlp", "req"),
        ),
        out_specs=(P(("req", "mlp"), None), P(None, "req", None, "mlp")),
        check_vma=False,
    )
```

profile of v0, /device:TPU:0, one launch (start us, length us, event | category | flops | bytes accessed | tf_op | source)
XLA Modules:
  0.0 720.8 jit_solution(13914493310342817437)
XLA Ops:
  8.1 2.6 fusion.93
  10.7 0.8 reduce-window.8
  11.7 1.1 convert_reduce_fusion.2
  12.9 1.2 fusion.48
  14.1 2.1 fusion.51
  16.2 11.0 %copy.88 = bf16[4,2,16,4096]{2,0,1,3:T(4,128)(2,1)} copy(bf16[4,2,16,4096]{3,2,1,0:T(8,128)(2,1)} %param.22) | data formatting | bytes 2097152 | tf_op args[6]
  27.2 11.3 %reshape.439 = bf16[8,2,32768]{2,1,0:T(2,128)(2,1)} reshape(bf16[4096,2,4,16]{3,2,1,0:T(4,128)(2,1)} %bitcast.123) | data formatting | bytes 2097152
  38.5 5.2 all-to-all-start
  45.1 0.7 fusion.96
  45.8 2.5 compare_select_fusion.10
  48.7 0.8 copy.94
  50.8 0.7 broadcast_compare_fusion.1
  51.5 8.3 %all-to-all-done = bf16[8,2,32768]{2,1,0:T(2,128)(2,1)S(1)} async-done(((bf16[8,2,32768]{2,1,0:T(2,128)(2,1)}), bf16[8,2,32768]{2,1,0:T(2,128)(2,1)S(1)}, u32[]{:S(2)}, u32[]{:S(2)}) %all-to-all-start) | async-done | bytes 1048608 | tf_op jit(solution)/shard_map/all_to_all | solution.py:126
  59.8 7.6 %reshape.440 = bf16[4096,2,4,16]{3,2,1,0:T(4,128)(2,1)} reshape(bf16[8,2,32768]{2,1,0:T(2,128)(2,1)S(1)} %all-to-all-done) | data formatting | bytes 2097152
  67.3 10.8 %copy.106 = bf16[4,2,16,8,512]{4,2,1,0,3:T(8,128)(2,1)S(1)} copy(bf16[4,2,16,8,512]{2,0,1,4,3:T(4,128)(2,1)} %bitcast.122) | data formatting | bytes 2097152 | tf_op jit(solution)/shard_map/all_to_all | solution.py:126
  78.2 2.7 fusion.99
  81.0 22.3 %psum.28 = bf16[256,32]{0,1:T(8,128)(2,1)S(1)} all-reduce(bf16[256,32]{0,1:T(8,128)(2,1)S(1)} %multiply_reduce_fusion.3), channel_id=1, replica_groups=mesh['req'=4,'mlp'=8] {'mlp'}, use_global_device_ids=true, to_apply=%region_5.6 | all-reduce | flops 8192 | bytes 32768 | tf_op jit(solution)/shard_map/psum | solution.py:120
  103.3 1.6 multiply_convert_fusion.1
  104.9 4.9 fusion.7
  110.3 4.1 multiply_reduce_fusion.1
  114.4 12.0 %all-reduce = (bf16[256]{0:T(256)(128)(2,1)S(1)}, bf16[256]{0:T(256)(128)(2,1)S(1)}) all-reduce(bf16[256]{0:T(256)(128)(2,1)S(1)} %get-tuple-element.62, bf16[256]{0:T(256)(128)(2,1)S(1)} %get-tuple-element.64), channel_id=1, replica_groups=mesh['req'=4,'mlp'=8] {'mlp'}, use_global_device_ids=true, to_apply=%region_9.10 | all-reduce | flops 512 | bytes 2048 | tf_op jit(solution)/shard_map/psum | solution.py:120
  127.7 4.8 fusion.9
  132.9 0.8 copy.107
  134.7 1.3 convolution_convert_fusion.3
  136.1 5.6 convolution_convert_fusion.2
  141.7 1.2 fusion.94
  142.9 42.6 %reduce-scatter.4.cloned.1.call-done = bf16[32,5120]{1,0:T(8,128)(2,1)} async-done(((bf16[256,5120]{1,0:T(8,128)(2,1)}), bf16[32,5120]{1,0:T(8,128)(2,1)}) %reduce-scatter.4.cloned.1.call-update) | async-done | bytes 327696 | tf_op jit(solution)/shard_map/reduce_scatter | solution.py:112
  185.5 1.4 convert_reduce_fusion.1
  187.1 0.9 fusion.47
  188.1 4.0 fusion.89
  192.1 4.0 reshape_squeeze.14
  196.1 2.1 reshape.438
  198.6 19.7 %all-gather.8.cloned.1.call-done = bf16[256,5120]{1,0:T(8,128)(2,1)} async-done(((bf16[32,5120]{1,0:T(8,128)(2,1)}), bf16[256,5120]{1,0:T(8,128)(2,1)}) %all-gather.8.cloned.1.call-update) | async-done | bytes 2621456 | tf_op jit(solution)/shard_map/all_gather | solution.py:109
  218.3 5.6 multiply_reduce_fusion
  223.9 13.3 %psum.31 = bf16[256]{0:T(256)(128)(2,1)S(1)} all-reduce(bf16[256]{0:T(256)(128)(2,1)S(1)} %get-tuple-element.66), channel_id=1, replica_groups=mesh['req'=4,'mlp'=8] {'mlp'}, use_global_device_ids=true, to_apply=%region_15.16 | all-reduce | flops 256 | bytes 1024 | tf_op jit(solution)/shard_map/psum | solution.py:120
  237.3 6.4 fusion
  243.6 5.9 fusion.24
  249.6 3.1 convolution_convert_fusion.1
  254.0 42.6 %reduce-scatter.6.cloned.1.call-done = bf16[32,5120]{1,0:T(8,128)(2,1)} async-done(((bf16[256,5120]{1,0:T(8,128)(2,1)}), bf16[32,5120]{1,0:T(8,128)(2,1)}) %reduce-scatter.6.cloned.1.call-update) | async-done | bytes 327696 | tf_op jit(solution)/shard_map/reduce_scatter | solution.py:112
  296.6 1.2 convert_reduce_fusion
  298.1 1.1 fusion.44
  299.6 139.0 %all-gather.12.cloned.1.call-done = bf16[5120,1024]{1,0:T(8,128)(2,1)} async-done(((bf16[1280,1024]{1,0:T(8,128)(2,1)}), bf16[5120,1024]{1,0:T(8,128)(2,1)}) %all-gather.12.cloned.1.call-update) | async-done | bytes 10485776 | tf_op jit(solution)/shard_map/all_gather | solution.py:123
  438.6 183.4 %all-gather.14.cloned.1.call-done = bf16[1024,5120]{1,0:T(8,128)(2,1)} async-done(((bf16[1024,1280]{1,0:T(8,128)(2,1)}), bf16[1024,5120]{1,0:T(8,128)(2,1)}) %all-gather.14.cloned.1.call-update) | async-done | bytes 10485776 | tf_op jit(solution)/shard_map/all_gather | solution.py:124
  622.0 30.5 %all-gather.10.cloned.1.call-done = bf16[256,5120]{1,0:T(8,128)(2,1)} async-done(((bf16[32,5120]{1,0:T(8,128)(2,1)}), bf16[256,5120]{1,0:T(8,128)(2,1)}) %all-gather.10.cloned.1.call-update) | async-done | bytes 2621456 | tf_op jit(solution)/shard_map/all_gather | solution.py:109
  652.5 15.1 %convolution_convert_fusion = bf16[256,5120]{1,0:T(8,128)(2,1)} fusion(bf16[1024,5120]{1,0:T(8,128)(2,1)} %all-gather.14.cloned.1.call-done, bf16[256,5120]{1,0:T(8,128)(2,1)} %all-gather.10.cloned.1.call-done, bf16[5120,1024]{1,0:T(8,128)(2,1)} %all-gather.12.cloned.1.call-done), kind=kOutput, calls=%fused_computation.6 | convolution fusion | flops 5372379136 | bytes 26214400 | tf_op jit(solution)/shard_map/dot_general | solution.py:257
  668.2 1.2 scatter_fusion
  669.5 42.0 %reduce-scatter.8.cloned.1.call-done = bf16[32,5120]{1,0:T(8,128)(2,1)} async-done(((bf16[256,5120]{1,0:T(8,128)(2,1)}), bf16[32,5120]{1,0:T(8,128)(2,1)}) %reduce-scatter.8.cloned.1.call-update) | async-done | bytes 327696 | tf_op jit(solution)/shard_map/reduce_scatter | solution.py:112
  711.5 2.0 fusion.54
  (150 shorter events, 9.5 us)
Async XLA Ops:
  8.0 70.2 %copy-start = (bf16[4,5120,32]{1,2,0:T(8,128)(2,1)S(1)}, bf16[4,5120,32]{1,2,0:T(8,128)(2,1)}, u32[]{:S(2)}) copy-start(bf16[4,5120,32]{1,2,0:T(8,128)(2,1)} %param.21) | copy-start | bytes 3932164
  8.0 70.2 %all-gather.6.cloned.1.call-start = ((), (), s32[]{:S(2)}) async-start(), calls=%async_computation.4 | async-start | bytes 2949120 | tf_op jit(solution)/shard_map/all_gather | solution.py:109
  11.7 15.5 %copy-start.27 = (pred[32]{0:T(512)(128)(4,1)}, pred[32]{0:T(512)(128)(4,1)S(1)}, u32[]{:S(2)}) copy-start(pred[32]{0:T(512)(128)(4,1)S(1)} %get-tuple-element.60) | copy-start | bytes 100
  11.7 15.5 %copy-start.29 = (pred[32]{0:T(512)(128)(4,1)}, pred[32]{0:T(512)(128)(4,1)S(1)}, u32[]{:S(2)}) copy-start(pred[32]{0:T(512)(128)(4,1)S(1)} %get-tuple-element.61) | copy-start | bytes 100
  27.2 16.5 %copy-start.34 = (s32[3,256]{1,0:T(4,128)S(1)}, s32[3,256]{1,0:T(4,128)}, u32[]{:S(2)}) copy-start(s32[3,256]{1,0:T(4,128)} %param.25) | copy-start | bytes 9220
  27.2 16.6 %copy-start.36 = (s32[4]{0:T(128)S(1)}, s32[4]{0:T(128)}, u32[]{:S(2)}) copy-start(s32[4]{0:T(128)} %param.19) | copy-start | bytes 52
  27.2 16.6 %copy-start.2 = (s32[32]{0:T(128)S(1)}, s32[32]{0:T(128)}, u32[]{:S(2)}) copy-start(s32[32]{0:T(128)} %param.20) | copy-start | bytes 388
  27.2 22.4 %copy-start.33 = (f32[3,512]{1,0:T(4,128)S(1)}, f32[3,512]{1,0:T(4,128)}, u32[]{:S(2)}) copy-start(f32[3,512]{1,0:T(4,128)} %param.24) | copy-start | bytes 18436
  38.5 21.3 %all-to-all-start = ((bf16[8,2,32768]{2,1,0:T(2,128)(2,1)}), bf16[8,2,32768]{2,1,0:T(2,128)(2,1)S(1)}, u32[]{:S(2)}, u32[]{:S(2)}) async-start(bf16[8,2,32768]{2,1,0:T(2,128)(2,1)} %reshape.439), calls=%async_computation | async-start | bytes 2097152 | tf_op jit(solution)/shard_map/all_to_all | solution.py:126
  43.7 141.8 %reduce-scatter.4.cloned.1.call-start = ((), (), s32[]{:S(2)}) async-start(), calls=%async_computation.5 | async-start | bytes 2949120 | tf_op jit(solution)/shard_map/reduce_scatter | solution.py:112
  104.9 5.3 copy-start.4
  110.3 16.2 %copy-start.32 = (f32[1,512]{1,0:T(1,128)S(1)}, f32[1,512]{1,0:T(1,128)}, u32[]{:S(2)}) copy-start(f32[1,512]{1,0:T(1,128)} %get-tuple-element.54) | copy-start | bytes 6148
  110.3 16.8 %copy-start.31 = (f32[1,512]{1,0:T(1,128)S(1)}, f32[1,512]{1,0:T(1,128)}, u32[]{:S(2)}) copy-start(f32[1,512]{1,0:T(1,128)} %get-tuple-element.53) | copy-start | bytes 6148
  127.7 4.9 copy-start.13
  127.7 6.1 copy-start.12
  132.9 3.1 copy-start.5
  136.0 49.5 %copy-start.3 = (bf16[32,5120]{1,0:T(8,128)(2,1)S(1)}, bf16[32,5120]{1,0:T(8,128)(2,1)}, u32[]{:S(2)}) copy-start(bf16[32,5120]{1,0:T(8,128)(2,1)} %param.16) | copy-start | bytes 983044
  136.0 49.4 %copy-start.25 = (f32[1,1,5120]{2,0,1:T(1,128)S(1)}, f32[1,1,5120]{2,0,1:T(1,128)}, u32[]{:S(2)}) copy-start(f32[1,1,5120]{2,0,1:T(1,128)} %get-tuple-element.40) | copy-start | bytes 61444
  136.0 49.4 %copy-start.28 = (pred[32]{0:T(512)(128)(4,1)S(1)}, pred[32]{0:T(512)(128)(4,1)}, u32[]{:S(2)}) copy-start(pred[32]{0:T(512)(128)(4,1)} %copy-done.27) | copy-start | bytes 100
  136.0 49.4 %copy-start.30 = (pred[32]{0:T(512)(128)(4,1)S(1)}, pred[32]{0:T(512)(128)(4,1)}, u32[]{:S(2)}) copy-start(pred[32]{0:T(512)(128)(4,1)} %copy-done.29) | copy-start | bytes 100
  136.1 51.1 %copy-start.26 = (f32[5120]{0:T(1024)S(1)}, f32[5120]{0:T(1024)}, u32[]{:S(2)}) copy-start(f32[5120]{0:T(1024)} %param.28) | copy-start | bytes 61444
  141.7 76.6 %all-gather.8.cloned.1.call-start = ((), (), s32[]{:S(2)}) async-start(), calls=%async_computation.6 | async-start | bytes 2949120 | tf_op jit(solution)/shard_map/all_gather | solution.py:109
  188.1 108.6 %reduce-scatter.6.cloned.1.call-start = ((), (), s32[]{:S(2)}) async-start(), calls=%async_computation.7 | async-start | bytes 2949120 | tf_op jit(solution)/shard_map/reduce_scatter | solution.py:112
  198.6 38.6 %copy-start.10 = (bf16[2048,4,128]{2,1,0:T(4,128)(2,1)S(1)}, bf16[2048,4,128]{2,1,0:T(4,128)(2,1)}, u32[]{:S(2)}) copy-start(bf16[2048,4,128]{2,1,0:T(4,128)(2,1)} %reshape_squeeze.14) | copy-start | bytes 6291460
  198.6 38.6 %copy-start.35 = (f32[1,512]{1,0:T(1,128)S(1)}, f32[1,512]{1,0:T(1,128)}, u32[]{:S(2)}) copy-start(f32[1,512]{1,0:T(1,128)} %get-tuple-element.52) | copy-start | bytes 6148
  237.2 6.4 copy-start.9
  237.2 12.3 %slice-start = ((s8[10485760]{0:T(1024)(128)(4,1)}), s8[4194304]{0:T(1024)(128)(4,1)S(1)}, s32[]{:S(2)}) async-start(s8[10485760]{0:T(1024)(128)(4,1)} %bitcast.159), calls=%async_computation.12 | async-start | bytes 8388608
  243.6 5.9 slice-start.1
  243.6 5.9 slice-start.2
  252.7 45.3 %copy-start.15 = (f32[1,1,5120]{2,0,1:T(1,128)S(1)}, f32[1,1,5120]{2,0,1:T(1,128)}, u32[]{:S(2)}) copy-start(f32[1,1,5120]{2,0,1:T(1,128)} %get-tuple-element.23) | copy-start | bytes 61444
  252.7 45.3 %copy-start.16 = (f32[1,1,5120]{2,0,1:T(1,128)S(1)}, f32[1,1,5120]{2,0,1:T(1,128)}, u32[]{:S(2)}) copy-start(f32[1,1,5120]{2,0,1:T(1,128)} %get-tuple-element.24) | copy-start | bytes 61444
  252.7 45.4 %copy-start.17 = (f32[1,1,5120]{2,0,1:T(1,128)S(1)}, f32[1,1,5120]{2,0,1:T(1,128)}, u32[]{:S(2)}) copy-start(f32[1,1,5120]{2,0,1:T(1,128)} %get-tuple-element.25) | copy-start | bytes 61444
  252.7 45.4 %copy-start.18 = (f32[1,1,5120]{2,0,1:T(1,128)S(1)}, f32[1,1,5120]{2,0,1:T(1,128)}, u32[]{:S(2)}) copy-start(f32[1,1,5120]{2,0,1:T(1,128)} %get-tuple-element.26) | copy-start | bytes 61444
  252.8 45.4 %copy-start.19 = (f32[1,1,5120]{2,0,1:T(1,128)S(1)}, f32[1,1,5120]{2,0,1:T(1,128)}, u32[]{:S(2)}) copy-start(f32[1,1,5120]{2,0,1:T(1,128)} %get-tuple-element.27) | copy-start | bytes 61444
  252.8 45.4 %copy-start.20 = (f32[1,1,5120]{2,0,1:T(1,128)S(1)}, f32[1,1,5120]{2,0,1:T(1,128)}, u32[]{:S(2)}) copy-start(f32[1,1,5120]{2,0,1:T(1,128)} %get-tuple-element.28) | copy-start | bytes 61444
  252.8 185.8 %all-gather.12.cloned.1.call-start = ((), (), s32[]{:S(2)}) async-start(), calls=%async_computation.9 | async-start | bytes 13107200 | tf_op jit(solution)/shard_map/all_gather | solution.py:123
  253.4 368.7 %all-gather.14.cloned.1.call-start = ((), (), s32[]{:S(2)}) async-start(), calls=%async_computation.10 | async-start | bytes 13107200 | tf_op jit(solution)/shard_map/all_gather | solution.py:124
  254.0 398.6 %all-gather.10.cloned.1.call-start = ((), (), s32[]{:S(2)}) async-start(), calls=%async_computation.8 | async-start | bytes 2949120 | tf_op jit(solution)/shard_map/all_gather | solution.py:109
  299.3 368.4 %copy-start.37 = (s32[1,16]{1,0:T(1,128)S(1)}, s32[1,16]{1,0:T(1,128)}, u32[]{:S(2)}) copy-start(s32[1,16]{1,0:T(1,128)} %param.26) | copy-start | bytes 196
  299.3 368.4 %copy-start.8 = (bf16[256,4,128]{2,0,1:T(8,128)(2,1)S(1)}, bf16[256,4,128]{2,0,1:T(8,128)(2,1)}, u32[]{:S(2)}) copy-start(bf16[256,4,128]{2,0,1:T(8,128)(2,1)} %copy-done.7) | copy-start | bytes 786436
  299.3 368.8 %copy-start.6 = (bf16[256,512]{1,0:T(8,128)(2,1)S(1)}, bf16[256,512]{1,0:T(8,128)(2,1)}, u32[]{:S(2)}) copy-start(bf16[256,512]{1,0:T(8,128)(2,1)} %copy-done.5) | copy-start | bytes 786436
  299.3 412.2 %reduce-scatter.8.cloned.1.call-start = ((), (), s32[]{:S(2)}) async-start(), calls=%async_computation.11 | async-start | bytes 2949120 | tf_op jit(solution)/shard_map/reduce_scatter | solution.py:112
  652.5 61.0 %copy-start.1 = (bf16[4,5120,32]{1,2,0:T(8,128)(2,1)S(1)}, bf16[4,5120,32]{1,2,0:T(8,128)(2,1)}, u32[]{:S(2)}) copy-start(bf16[4,5120,32]{1,2,0:T(8,128)(2,1)} %param.21) | copy-start | bytes 3932164
  667.7 43.8 %copy-start.21 = (f32[1,1,5120]{2,0,1:T(1,128)S(1)}, f32[1,1,5120]{2,0,1:T(1,128)}, u32[]{:S(2)}) copy-start(f32[1,1,5120]{2,0,1:T(1,128)} %get-tuple-element.22) | copy-start | bytes 61444
  667.7 43.8 %copy-start.22 = (f32[1,1,5120]{2,0,1:T(1,128)S(1)}, f32[1,1,5120]{2,0,1:T(1,128)}, u32[]{:S(2)}) copy-start(f32[1,1,5120]{2,0,1:T(1,128)} %get-tuple-element.29) | copy-start | bytes 61444
  667.7 43.8 %copy-start.23 = (f32[1,1,5120]{2,0,1:T(1,128)S(1)}, f32[1,1,5120]{2,0,1:T(1,128)}, u32[]{:S(2)}) copy-start(f32[1,1,5120]{2,0,1:T(1,128)} %get-tuple-element.30) | copy-start | bytes 61444
  667.7 43.9 %copy-start.24 = (f32[1,1,5120]{2,0,1:T(1,128)S(1)}, f32[1,1,5120]{2,0,1:T(1,128)}, u32[]{:S(2)}) copy-start(f32[1,1,5120]{2,0,1:T(1,128)} %get-tuple-element.31) | copy-start | bytes 61444
  669.5 44.0 %copy-start.11 = (bf16[2,16,16,512]{3,2,1,0:T(8,128)(2,1)}, bf16[2,16,16,512]{3,2,1,0:T(8,128)(2,1)S(1)}, u32[]{:S(2)}) copy-start(bf16[2,16,16,512]{3,2,1,0:T(8,128)(2,1)S(1)} %scatter_fusion) | copy-start | bytes 1572868
  (2 other events, 3.6 us)
Sparse Core Ops, SparseCore 0:
  16.3 33.5 all-gather.5
  141.8 43.6 reduce-scatter.3
  188.2 30.0 all-gather.7
  252.9 43.6 reduce-scatter.5
  667.8 43.6 reduce-scatter.7
Sparse Core Ops, SparseCore 1:
  254.8 183.7 all-gather.11
  440.1 181.9 all-gather.13
  624.4 28.1 all-gather.9
where the time goes:
time: 723 us; the launch traced here: 721 us
  waiting for transfers between devices  509 us (70%)
  local copies, waits for them, and re-layouts  61.7 us (9%)
  matrix products  60.8 us (8%)
  blocking collectives  47.6 us (7%)
  other arithmetic  19.5 us (3%)
  between operations  16.2 us (2%)
    all_gather x1, waiting for transfers between devices, body(): lax.all_gather(feedforward_down, 'req', axis=1, tiled=True)  183 us
    all_gather x1, waiting for transfers between devices, body(): lax.all_gather(feedforward_up, 'req', axis=0, tiled=True)  139 us
    reduce_scatter x3, waiting for transfers between devices, sum_rows(): lax.psum_scatter(term_fn(jnp.int32(0), own_count * lax.axis_size('mlp'))....  127 us
    all_gather x3, waiting for transfers between devices, over_group(): lax.all_gather(own_rows, 'mlp', axis=0, tiled=True)  50.2 us
    psum x3, blocking collectives, global_sum(): lax.psum(as_sent(pieces), 'mlp')  47.6 us
    unnamed x85, local copies, waits for them, and re-layouts  30 us
    dot_general x1, matrix products, down_term(): return jnp.dot(hidden, down_full, preferred_element_type=jnp.float32)  15.1 us
  transfers between devices with their start and end apart: 9, of which 8 were waited for; matrix products, arithmetic and copies ran while one was open for 9% of the time, Pallas kernels for 0%

commit v1 on v0

v1 whole, which is shorter than its diff:
```python
import functools
import math

import jax
import jax.numpy as jnp
from jax import lax
from jax.experimental import pallas as pl
from jax.experimental.pallas import tpu as pltpu
from jax.sharding import PartitionSpec as P

HD = 128
PAGE = 16


EPSILON = 1e-06


PAIR = 2
MESH = pl.DeviceIdType.MESH
ANY = pl.BlockSpec(memory_space=pl.ANY)
VM = pl.BlockSpec(memory_space=pltpu.VMEM)


def comm_call(kernel, out_shape, in_specs, out_specs, scratch, ident):
    return pl.pallas_call(
        kernel,
        out_shape=out_shape,
        in_specs=in_specs,
        out_specs=out_specs,
        scratch_shapes=scratch,
        compiler_params=pltpu.CompilerParams(
            collective_id=ident, has_side_effects=True, vmem_limit_bytes=48 << 20
        ),
    )


def remote(source, target, send_sem, recv_sem, axis, place):
    return pltpu.make_async_remote_copy(
        src_ref=source,
        dst_ref=target,
        send_sem=send_sem,
        recv_sem=recv_sem,
        device_id={axis: place},
        device_id_type=MESH,
    )


def shift(me, step, count):
    return lax.rem(me + (step + count) % count, count)


def greet(peers):
    barrier = pltpu.get_barrier_semaphore()
    for axis, place in peers:
        pl.semaphore_signal(barrier, inc=1, device_id={axis: place}, device_id_type=MESH)
    pl.semaphore_wait(barrier, len(peers))


def pair_places(count):
    me = lax.axis_index("mlp")
    outer, core = lax.div(me, PAIR), lax.rem(me, PAIR)
    sibling = outer * PAIR + (PAIR - 1 - core)
    peers = [
        shift(outer, k, count // PAIR) * PAIR + core for k in range(count // PAIR)
    ]
    sources = [
        shift(outer, -k, count // PAIR) * PAIR + core for k in range(count // PAIR)
    ]
    return me, core, sibling, peers, sources


def gather_sems(count):
    steps = count // PAIR
    return [pltpu.SemaphoreType.DMA(())] + [pltpu.SemaphoreType.DMA((steps,))] * 4


def gather_rows(count, places, own_ref, out_ref, own_sem, send_sem, recv_sem, pass_send, pass_recv):
    me, core, sibling, peers, sources = places
    own = pltpu.make_async_copy(own_ref, out_ref.at[me], own_sem)
    sends = [
        remote(own_ref, out_ref.at[me], send_sem.at[k], recv_sem.at[k], "mlp", peers[k])
        for k in range(1, count // PAIR)
    ]
    for copy in sends:
        copy.start()
    passes = [remote(own_ref, out_ref.at[me], pass_send.at[0], pass_recv.at[0], "mlp", sibling)]
    passes[0].start()
    own.start()
    for k in range(1, count // PAIR):
        sends[k - 1].wait_recv()
        block = out_ref.at[sources[k]]
        passes.append(remote(block, block, pass_send.at[k], pass_recv.at[k], "mlp", sibling))
        passes[-1].start()
    for copy in sends:
        copy.wait_send()
    for copy in passes:
        copy.wait()
    own.wait()


def entry_kernel(count, tok_ref, scale_ref, shift_ref, maps_ref, out_ref, up_ref, norm, map_own, map_send, map_recv, *sems):
    places = pair_places(count)
    me = places[0]
    slots, width = maps_ref.shape[0], up_ref.shape[-1]
    others = [shift(me, k, count) for k in range(1, count)]
    greet([("mlp", place) for place in others])

    def columns(place):
        return maps_ref.at[:, :, :, pl.ds(pl.multiple_of(place * width, 128), width)]

    target = up_ref.at[pl.ds(me * slots, slots)]
    own = pltpu.make_async_copy(columns(me), target, map_own)
    own.start()
    copies = [
        remote(columns(place), target, map_send.at[k], map_recv.at[k], "mlp", place)
        for k, place in enumerate(others)
    ]
    norm[...] = (
        layer_norm(tok_ref[...].astype(jnp.float32)) * (1.0 + scale_ref[...]) + shift_ref[...]
    ).astype(jnp.bfloat16)
    for copy in copies:
        copy.start()
    gather_rows(count, places, norm, out_ref, *sems)
    for copy in copies:
        copy.wait()
    own.wait()


def entry_rows(tokens, scale, shift_rows, maps, count):
    rows, width = tokens.shape
    slots, two, rank, total = maps.shape
    dma = pltpu.SemaphoreType.DMA
    gathered, up = comm_call(
        functools.partial(entry_kernel, count),
        (
            jax.ShapeDtypeStruct((count, rows, width), jnp.bfloat16),
            jax.ShapeDtypeStruct((count * slots, two, rank, total // count), maps.dtype),
        ),
        [VM, VM, VM, ANY],
        (ANY, ANY),
        [pltpu.VMEM((rows, width), jnp.bfloat16), dma(()), dma((count - 1,)), dma((count - 1,))]
        + gather_sems(count),
        0,
    )(tokens, scale, shift_rows, maps)
    return gathered.reshape(count * rows, width), up


def sum_blocks(count, places, block_of, near, mid, far, ns, nr, fs, fr):
    me, core, sibling, peers, sources = places
    steps = count // PAIR
    order = list(range(1, steps)) + [0]
    pairs = {}
    for k in order:
        other = peers[k] + (PAIR - 1 - 2 * core)
        pairs[k] = remote(block_of(other), near.at[k], ns.at[k], nr.at[k], "mlp", sibling)
        pairs[k].start()
    sends = []
    for k in range(1, steps):
        pairs[k].wait_recv()
        mid[k] = (
            block_of(peers[k])[...].astype(jnp.float32) + near[k].astype(jnp.float32)
        ).astype(jnp.bfloat16)
        sends.append(remote(mid.at[k], far.at[k], fs.at[k], fr.at[k], "mlp", peers[k]))
        sends[-1].start()
    pairs[0].wait_recv()
    total = block_of(me)[...].astype(jnp.float32) + near[0].astype(jnp.float32)
    for k in range(1, steps):
        sends[k - 1].wait_recv()
        total = total + far[k].astype(jnp.float32)
    for k in order:
        pairs[k].wait_send()
    for copy in sends:
        copy.wait_send()
    return total


def sum_scratch(count, extent):
    steps = count // PAIR
    return [pltpu.VMEM((steps,) + extent, jnp.bfloat16)] * 3 + [
        pltpu.SemaphoreType.DMA((steps,))
    ] * 4


def middle_kernel(count, part_ref, base_ref, gate_ref, scale_ref, shift_ref, res_ref, out_ref, near, mid, far, norm, ns, nr, fs, fr, *sems):
    places = pair_places(count)
    greet([("mlp", places[2])] + [("mlp", place) for place in places[3][1:]])
    total = sum_blocks(
        count, places, lambda place: part_ref.at[place], near, mid, far, ns, nr, fs, fr
    )
    res = (base_ref[...].astype(jnp.float32) + gate_ref[...] * total).astype(jnp.bfloat16)
    res_ref[...] = res
    norm[...] = (layer_norm(res.astype(jnp.float32)) * scale_ref[...] + shift_ref[...]).astype(
        jnp.bfloat16
    )
    gather_rows(count, places, norm, out_ref, *sems)


def middle_rows(part, base, gate, scale, shift_rows, count, ident):
    rows, width = base.shape
    scratch = sum_scratch(count, (rows, width))
    res, gathered = comm_call(
        functools.partial(middle_kernel, count),
        (
            jax.ShapeDtypeStruct((rows, width), jnp.bfloat16),
            jax.ShapeDtypeStruct((count, rows, width), jnp.bfloat16),
        ),
        [VM] * 5,
        (VM, ANY),
        scratch[:3] + [pltpu.VMEM((rows, width), jnp.bfloat16)] + scratch[3:] + gather_sems(count),
        ident,
    )(part.reshape(count, rows, width), base, gate, scale, shift_rows)
    return res, gathered.reshape(count * rows, width)


def small_kernel(count, own_ref, out_ref, slots, send_sem, recv_sem):
    me = lax.axis_index("mlp")
    others = [shift(me, k, count) for k in range(1, count)]
    greet([("mlp", place) for place in others])
    copies = [
        remote(own_ref, slots.at[k], send_sem.at[k], recv_sem.at[k], "mlp", place)
        for k, place in enumerate(others)
    ]
    for copy in copies:
        copy.start()
    total = own_ref[...].astype(jnp.float32)
    for k, copy in enumerate(copies):
        copy.wait_recv()
        total = total + slots[k].astype(jnp.float32)
    out_ref[...] = total
    for copy in copies:
        copy.wait_send()


def small_sum(own, count, ident):
    dma = pltpu.SemaphoreType.DMA((count - 1,))
    return comm_call(
        functools.partial(small_kernel, count),
        jax.ShapeDtypeStruct(own.shape, jnp.float32),
        [VM],
        VM,
        [pltpu.VMEM((count - 1,) + own.shape, own.dtype), dma, dma],
        ident,
    )(own)


def line_kernel(count, own_ref, out_ref, own_sem, rs, rr, ls, lr):
    me = lax.axis_index("req")
    right, left = shift(me, 1, count), shift(me, -1, count)
    greet([("req", right), ("req", left)])
    own = pltpu.make_async_copy(own_ref, out_ref.at[me], own_sem)
    own.start()

    def hop(step, sign):
        block = jnp.clip(me - sign * step, 0, count - 1)
        source = own_ref if step == 0 else out_ref.at[block]
        send, recv, place = (rs, rr, right) if sign > 0 else (ls, lr, left)
        return remote(source, out_ref.at[block], send.at[step], recv.at[step], "req", place)

    for step in range(count - 1):
        if step > 0:

            @pl.when(me >= step)
            def _():
                hop(step - 1, 1).wait_recv()

            @pl.when(me + step < count)
            def _():
                hop(step - 1, -1).wait_recv()

        @pl.when((me >= step) & (me < count - 1))
        def _():
            hop(step, 1).start()

        @pl.when((me + step < count) & (me > 0))
        def _():
            hop(step, -1).start()

    @pl.when(me >= count - 1)
    def _():
        hop(count - 2, 1).wait_recv()

    @pl.when(me < 1)
    def _():
        hop(count - 2, -1).wait_recv()

    for step in range(count - 1):

        @pl.when((me >= step) & (me < count - 1))
        def _():
            hop(step, 1).wait_send()

        @pl.when((me + step < count) & (me > 0))
        def _():
            hop(step, -1).wait_send()

    own.wait()


def line_gather(own, count, ident):
    dma = pltpu.SemaphoreType.DMA
    return comm_call(
        functools.partial(line_kernel, count),
        jax.ShapeDtypeStruct((count,) + own.shape, own.dtype),
        [ANY],
        ANY,
        [dma(())] + [dma((count - 1,))] * 4,
        ident,
    )(own)


def exit_kernel(count, lines, part_ref, out_ref, near, mid, far, final, ns, nr, fs, fr, own_sem, send_sem, recv_sem):
    places = pair_places(count)
    line = lax.axis_index("req")
    others = [shift(line, k, lines) for k in range(1, lines)]
    greet(
        [("mlp", places[2])]
        + [("mlp", place) for place in places[3][1:]]
        + [("req", place) for place in others]
    )
    final[...] = sum_blocks(
        count, places, lambda place: part_ref.at[:, place], near, mid, far, ns, nr, fs, fr
    ).astype(jnp.bfloat16)
    width = final.shape[-1]
    target = out_ref.at[:, pl.ds(pl.multiple_of(line * width, 128), width)]
    own = pltpu.make_async_copy(final.at[line], target, own_sem)
    own.start()
    copies = [
        remote(final.at[place], target, send_sem.at[k], recv_sem.at[k], "req", place)
        for k, place in enumerate(others)
    ]
    for copy in copies:
        copy.start()
    for copy in copies:
        copy.wait()
    own.wait()


def exit_rows(part, count, lines, ident):
    groups, _, rows, width = part.shape
    scratch = sum_scratch(count, (groups, rows, width))
    dma = pltpu.SemaphoreType.DMA
    return comm_call(
        functools.partial(exit_kernel, count, lines),
        jax.ShapeDtypeStruct((rows, lines * width), jnp.bfloat16),
        [VM],
        VM,
        scratch[:3]
        + [pltpu.VMEM((groups, rows, width), jnp.bfloat16)]
        + scratch[3:]
        + [dma(()), dma((lines - 1,)), dma((lines - 1,))],
        ident,
    )(part)


def layer_norm(values):
    center = values - jnp.mean(values, axis=-1, keepdims=True)
    spread = jnp.mean(center * center, axis=-1, keepdims=True)
    return center * lax.rsqrt(spread + EPSILON)


def rotary_tables(grid):
    half_dim = HD // 2
    spatial = half_dim // 3
    temporal = half_dim - 2 * spatial
    column = jnp.arange(half_dim, dtype=jnp.int32)
    which_axis = jnp.where(
        column < temporal, 0, jnp.where(column < temporal + spatial, 1, 2)
    ).astype(jnp.int32)
    offset = jnp.where(
        which_axis == 0, 0, jnp.where(which_axis == 1, temporal, temporal + spatial)
    ).astype(jnp.int32)
    span_size = jnp.where(which_axis == 0, temporal, spatial).astype(jnp.float32)
    frequency = jnp.exp(-(column - offset).astype(jnp.float32) / span_size * math.log(10000.0))
    coordinate = grid.astype(jnp.float32)[which_axis, :].T
    angles = coordinate * frequency[None, :]
    return (jnp.cos(angles), jnp.sin(angles))


def rotate(values, cosine, sine_part):
    half_dim = HD // 2
    front_half = values[..., :half_dim]
    back_half = values[..., half_dim:]
    cosine = cosine[:, None, :]
    sine_part = sine_part[:, None, :]
    return jnp.concatenate(
        [front_half * cosine - back_half * sine_part, back_half * cosine + front_half * sine_part],
        axis=-1,
    )


def attend(queries, key_rows, value_rows, allowed):
    scores = jnp.einsum(
        "thd,shd->hts", queries, key_rows, preferred_element_type=jnp.float32
    ) / math.sqrt(HD)
    scores = jnp.where(allowed[None], scores, -1e30)
    weights = jnp.exp(scores)
    weights = (weights / jnp.sum(weights, axis=-1, keepdims=True)).astype(jnp.bfloat16)
    return jnp.einsum(
        "hts,shd->thd", weights, value_rows, preferred_element_type=jnp.float32
    ).astype(jnp.bfloat16)


def choose_rows(table, segment):
    chosen = jnp.zeros((segment.shape[0],) + table.shape[1:], table.dtype)
    for request in range(table.shape[0]):
        picked = (segment == request).reshape((-1,) + (1,) * (table.ndim - 1))
        chosen = jnp.where(picked, table[request][None], chosen)
    return chosen


def body(
    tokens,
    modulation,
    lengths,
    request_adapter,
    adapter_storage,
    adapter_down_weight,
    adapter_up_maps,
    input_projection,
    query_key_gains,
    positions,
    block_page_lookup,
    output_projection,
    cross_norm_gain,
    text_token_cache,
    feedforward_up,
    feedforward_down,
):
    mlp_count = lax.axis_size("mlp")
    my_index = lax.axis_index("mlp")
    own_count = tokens.shape[0]
    group_rows = own_count * mlp_count
    local_width = input_projection.shape[2]
    heads_local = local_width // HD
    entire_width = local_width * mlp_count
    resident_slots = adapter_down_weight.shape[0]
    doubled_rank = adapter_down_weight.shape[2]
    rank_once = doubled_rank // 2

    req_count = lax.axis_size("req")
    slot_total = resident_slots * mlp_count
    up_full = lax.all_gather(feedforward_up, "req", axis=0, tiled=True)
    bounds = jnp.cumsum(lengths[0])
    position = jnp.arange(group_rows, dtype=jnp.int32)
    segment = jnp.sum((position[:, None] >= bounds[None, :]).astype(jnp.int32), axis=1)
    own_start = my_index * own_count
    own_segment = lax.dynamic_slice_in_dim(segment, own_start, own_count)
    per_token = [choose_rows(modulation[:, which_row, :], own_segment) for which_row in range(6)]
    token_f32 = tokens.astype(jnp.float32)
    rows_in, adapter_up_weight = entry_rows(
        tokens, per_token[1], per_token[0], adapter_up_maps, mlp_count
    )
    request_slot = adapter_storage[request_adapter]
    token_slot = choose_rows(request_slot, segment)
    resident = my_index * resident_slots + jnp.arange(resident_slots, dtype=jnp.int32)
    held = (token_slot[None, :] == resident[:, None]).astype(jnp.float32)
    code_block = lax.dot_general(
        adapter_down_weight.transpose(0, 2, 1).reshape(resident_slots * doubled_rank, -1),
        rows_in,
        (((1,), (1,)), ((), ())),
        preferred_element_type=jnp.float32,
    ).reshape(resident_slots, doubled_rank, group_rows)
    my_codes = jnp.sum(held[:, None, :] * code_block, axis=0).astype(jnp.bfloat16)
    codes = small_sum(my_codes, mlp_count, 1).astype(jnp.bfloat16)
    slots = jnp.arange(slot_total, dtype=jnp.int32)
    everywhere = token_slot[None, :] == slots[:, None]

    def spread(code_part):
        return jnp.where(everywhere[:, None, :], code_part[None], jnp.bfloat16(0)).reshape(
            slot_total * rank_once, group_rows
        )

    def adapted(code_part, which_map):
        return lax.dot_general(
            spread(code_part),
            adapter_up_weight[:, which_map].reshape(slot_total * rank_once, local_width),
            (((0,), (0,)), ((), ())),
            preferred_element_type=jnp.float32,
        )

    def project(which_map):
        return jnp.dot(rows_in, input_projection[which_map], preferred_element_type=jnp.float32)

    query_linear = project(0) + adapted(codes[:rank_once], 0)
    key_linear = project(1)
    value_rows = (project(2) + adapted(codes[rank_once:], 1)).astype(jnp.bfloat16)
    squares = small_sum(
        jnp.stack(
            [jnp.sum(query_linear * query_linear, axis=1), jnp.sum(key_linear * key_linear, axis=1)]
        ),
        mlp_count,
        2,
    )
    query_square, key_square = squares[0], squares[1]
    query_norm = (
        query_linear
        * lax.rsqrt(query_square / entire_width + EPSILON)[:, None]
        * query_key_gains[0]
    )
    key_norm = (
        key_linear * lax.rsqrt(key_square / entire_width + EPSILON)[:, None] * query_key_gains[1]
    )
    cosine, sine_part = rotary_tables(positions)
    query_rot = rotate(query_norm.reshape(group_rows, heads_local, HD), cosine, sine_part).astype(
        jnp.bfloat16
    )
    key_rot = rotate(key_norm.reshape(group_rows, heads_local, HD), cosine, sine_part).astype(
        jnp.bfloat16
    )
    value_heads = value_rows.reshape(group_rows, heads_local, HD)
    page_count = group_rows // PAGE
    stacked = jnp.stack(
        [
            key_rot.reshape(page_count, PAGE, local_width),
            value_rows.reshape(page_count, PAGE, local_width),
        ]
    )
    kv_pages = jnp.zeros_like(stacked).at[:, block_page_lookup[0]].set(stacked)
    allowed = segment[:, None] == segment[None, :]
    attended = attend(query_rot, key_rot, value_heads, allowed).reshape(group_rows, local_width)
    text_owner = (
        jnp.arange(text_token_cache.shape[1] * text_token_cache.shape[2], dtype=jnp.int32)
        // text_token_cache.shape[2]
    )
    cross_allowed = segment[:, None] == text_owner[None, :]
    text_keys = text_token_cache[0].reshape(-1, heads_local, HD)
    text_values = text_token_cache[1].reshape(-1, heads_local, HD)

    def out_rows(rows, which_map):
        return jnp.dot(
            rows, output_projection[which_map], preferred_element_type=jnp.float32
        ).astype(jnp.bfloat16)

    first_res, cross_in = middle_rows(
        out_rows(attended, 0),
        tokens,
        per_token[2],
        cross_norm_gain[None, :],
        jnp.zeros((1, tokens.shape[1]), jnp.float32),
        mlp_count,
        3,
    )
    cross_linear = jnp.dot(cross_in, input_projection[3], preferred_element_type=jnp.float32)
    cross_square = small_sum(
        jnp.sum(cross_linear * cross_linear, axis=1)[None, :], mlp_count, 4
    )[0]
    cross_query = (
        cross_linear
        * lax.rsqrt(cross_square / entire_width + EPSILON)[:, None]
        * query_key_gains[2]
    ).astype(jnp.bfloat16)
    cross_out = attend(
        cross_query.reshape(group_rows, heads_local, HD), text_keys, text_values, cross_allowed
    ).reshape(group_rows, local_width)

    second_res, mlp_in = middle_rows(
        out_rows(cross_out, 1),
        first_res,
        jnp.ones((1, tokens.shape[1]), jnp.float32),
        1.0 + per_token[4],
        per_token[3],
        mlp_count,
        5,
    )
    hidden = jax.nn.gelu(
        jnp.dot(mlp_in, up_full, preferred_element_type=jnp.float32), approximate=True
    ).astype(jnp.bfloat16)
    hidden_all = line_gather(hidden, req_count, 6)
    units, columns = feedforward_down.shape
    down_part = jnp.dot(
        hidden_all.reshape(req_count * group_rows, units),
        feedforward_down,
        preferred_element_type=jnp.float32,
    ).astype(jnp.bfloat16)
    down_own = exit_rows(
        down_part.reshape(req_count, mlp_count, own_count, columns), mlp_count, req_count, 7
    )
    layer_out = (
        second_res.astype(jnp.float32) + per_token[5] * down_own.astype(jnp.float32)
    ).astype(jnp.bfloat16)
    return (layer_out, kv_pages)


def solution(mesh):
    return jax.shard_map(
        body,
        mesh=mesh,
        in_specs=(
            P(("req", "mlp"), None),
            P("req", None, None),
            P("req", None),
            P("req"),
            P(),
            P("mlp", None, None),
            P("mlp", None, None, None),
            P(None, None, "mlp"),
            P(None, "mlp"),
            P(None, "req"),
            P("req", None),
            P(None, "mlp", None),
            P(),
            P(None, "req", None, "mlp"),
            P("req", "mlp"),
            P("mlp", "req"),
        ),
        out_specs=(P(("req", "mlp"), None), P(None, "req", None, "mlp")),
        check_vma=False,
    )
```

time: 723 us -> 329 us (0.46)
  waiting for transfers between devices: 509 us -> 0.68 us
  Pallas kernels: 0 us -> 196 us
  blocking collectives: 47.6 us -> 0 us
  local copies, waits for them, and re-layouts: 61.7 us -> 39.1 us
    all_gather x5 -> x1, waiting for transfers between devices: 373 us -> 0.01 us  [body(): up_full = lax.all_gather(feedforward_up, 'req', axis=0, tiled=True)]
    pallas_call x0 -> x8, Pallas kernels: none -> 196 us  [the longest x2 80.2 us: middle_rows(): comm_call(functools.partial(middle_kernel, count), (jax.ShapeDtypeStruct(...]
    reduce_scatter x3 -> x0, waiting for transfers between devices: 127 us -> none  [sum_rows(): lax.psum_scatter(term_fn(jnp.int32(0), own_count * lax.axis_size('mlp'))....]
    psum x3 -> x0, blocking collectives: 47.6 us -> none  [global_sum(): lax.psum(as_sent(pieces), 'mlp')]
    unnamed x85 -> x74, local copies, waits for them, and re-layouts: 30 us -> 3.47 us
    all_to_all x1 -> x0, local copies, waits for them, and re-layouts: 10.8 us -> none  [body(): lax.all_to_all(adapter_up_maps, 'mlp', split_axis=3, concat_axis=0, tiled...]
    all_to_all x1 -> x0, waiting for transfers between devices: 8.27 us -> none  [body(): lax.all_to_all(adapter_up_maps, 'mlp', split_axis=3, concat_axis=0, tiled...]
    dot_general x9 -> x11, matrix products: 44.1 us -> 42.5 us  [the longest x3 13.1 us: project(): jnp.dot(rows_in, input_projection[which_map], preferred_element_type=jnp....]
  transfers between devices with their start and end apart: 9 -> 1, of which waited for: 8 -> 0; matrix products, arithmetic and copies ran while one was open for 9% -> 31% of each run, Pallas kernels for 0% -> 39%
where the time goes in v1:
time: 329 us; the launch traced here: 328 us
  Pallas kernels  196 us (60%)
  matrix products  60.3 us (18%)
  local copies, waits for them, and re-layouts  39.1 us (12%)
  other arithmetic  17.2 us (5%)
  between operations  14.6 us (4%)
    pallas_call x2, Pallas kernels, middle_rows(): comm_call(functools.partial(middle_kernel, count), (jax.ShapeDtypeStruct(...  80.2 us
    pallas_call x1, Pallas kernels, line_gather(): comm_call(functools.partial(line_kernel, count), jax.ShapeDtypeStruct((co...  40.7 us
    pallas_call x1, Pallas kernels, entry_rows(): comm_call(functools.partial(entry_kernel, count), (jax.ShapeDtypeStruct((...  33.7 us
    pallas_call x1, Pallas kernels, exit_rows(): comm_call(functools.partial(exit_kernel, count, lines), jax.ShapeDtypeStr...  26.7 us
    pallas_call x3, Pallas kernels, small_sum(): comm_call(functools.partial(small_kernel, count), jax.ShapeDtypeStruct(ow...  14.7 us
    dot_general x3, matrix products, project(): jnp.dot(rows_in, input_projection[which_map], preferred_element_type=jnp....  13.1 us
    dot_general x2, matrix products, attend(): jnp.einsum('thd,shd->hts', queries, key_rows, preferred_element_type=jnp....  9.27 us
    dot_general x2, matrix products, out_rows(): jnp.dot(rows, output_projection[which_map], preferred_element_type=jnp.fl...  9.01 us
  transfers between devices with their start and end apart: 1, of which 0 were waited for; matrix products, arithmetic and copies ran while one was open for 31% of the time, Pallas kernels for 39%

profile of v1, /device:TPU:0, one launch (start us, length us, event | category | flops | bytes accessed | tf_op | source)
XLA Modules:
  0.0 328.1 jit_solution(10383278480468446883)
XLA Ops:
  7.9 4.6 %fusion.57 = (bf16[1,4,512,512]{3,2,1,0:T(8,128)(2,1)}, bf16[1,4,512,512]{3,2,1,0:T(8,128)(2,1)}) fusion(bf16[2,4,512,512]{3,2,1,0:T(8,128)(2,1)} %param.29), kind=kLoop, calls=%fused_computation.127 | loop fusion | bytes 8388608 | tf_op jit(solution)/shard_map/slice | solution.py:526
  12.5 4.0 %reshape.457 = bf16[2048,4,128]{2,1,0:T(4,128)(2,1)} reshape(bf16[1,4,512,512]{3,2,1,0:T(8,128)(2,1)} %get-tuple-element.17) | data formatting | bytes 4194304 | tf_op jit(solution)/shard_map/reshape;squeeze | solution.py:527
  16.8 4.0 %reshape_squeeze.14 = bf16[2048,4,128]{2,1,0:T(4,128)(2,1)} reshape(bf16[1,4,512,512]{3,2,1,0:T(8,128)(2,1)} %get-tuple-element.16) | data formatting | bytes 4194304 | tf_op jit(solution)/shard_map/reshape;squeeze | solution.py:526
  20.8 0.9 fusion.61
  23.2 1.1 select_add_fusion
  24.3 1.2 select_select_fusion
  25.5 1.0 copy-done.3
  26.5 33.7 %shard_map.167 = (bf16[8,32,5120]{2,1,0:T(8,128)(2,1)}, bf16[32,2,16,512]{3,2,1,0:T(8,128)(2,1)S(1)}) custom-call(bf16[32,5120]{1,0:T(8,128)(2,1)S(1)} %copy-done.3, f32[32,5120]{1,0:T(8,128)S(1)} %get-tuple-element.65.scale_ref, f32[32,5120]{1,0:T(8,128)S(1)} %get-tuple-element.62.shift_ref, bf16[4,2,16,4096]{3,2,1,0:T(8,128)(2,1)S(1)} %copy-done.5), custom_call_target="tpu_custom_call" | custom-call | tf_op jit(solution)/shard_map/pallas_call | solution.py:133
  60.9 2.5 compare_select_fusion.10
  63.5 2.9 fusion.66
  66.5 5.4 %shard_map.168 = f32[32,256]{1,0:T(8,128)S(1)} custom-call(bf16[32,256]{1,0:T(8,128)(2,1)S(1)} %multiply_reduce_fusion.3.own_ref), custom_call_target="tpu_custom_call" | custom-call | tf_op jit(solution)/shard_map/pallas_call | solution.py:236
  72.7 0.9 fusion.58
  73.5 4.0 %fusion.9 = f32[256,512]{1,0:T(8,128)S(1)} fusion(bf16[256,5120]{1,0:T(8,128)(2,1)S(1)} %bitcast.141, bf16[4,5120,512]{2,1,0:T(8,128)(2,1)} %param.23), kind=kOutput, calls=%fused_computation.16 | convolution fusion | flops 1342177280 | bytes 8388608 | tf_op jit(solution)/shard_map/dot_general | solution.py:482
  78.7 4.9 %fusion.7 = f32[256,512]{1,0:T(8,128)S(1)} fusion(bf16[256,5120]{1,0:T(8,128)(2,1)} %bitcast.140, bf16[4,5120,512]{2,1,0:T(8,128)(2,1)} %param.23), kind=kOutput, calls=%fused_computation.14 | convolution fusion | flops 1342177280 | bytes 8388608 | tf_op jit(solution)/shard_map/dot_general | solution.py:482
  83.7 1.1 multiply_reduce_fusion.2
  84.8 4.2 %multiply_reduce_fusion.1 = (f32[256]{0:T(256)S(1)}, f32[256,512]{1,0:T(8,128)S(1)}) fusion(bf16[256,5120]{1,0:T(8,128)(2,1)S(1)} %bitcast.142, bf16[4,5120,512]{2,1,0:T(8,128)(2,1)} %param.23), kind=kOutput, calls=%fused_computation.65 | convolution fusion | flops 1342439168 | bytes 8389632 | tf_op jit(solution)/shard_map/dot_general | solution.py:482
  89.0 4.7 %shard_map.169 = f32[2,256]{1,0:T(2,128)S(1)} custom-call(f32[2,256]{1,0:T(2,128)S(1)} %pad_maximum_fusion.own_ref), custom_call_target="tpu_custom_call" | custom-call | tf_op jit(solution)/shard_map/pallas_call | solution.py:236
  94.9 0.9 multiply_multiply_fusion.1
  95.8 2.0 reshape.422
  99.1 1.4 gather_fusion.1
  100.5 1.8 cosine_bitcast_fusion
  102.3 1.6 copy.45
  103.9 1.6 copy.43
  105.5 2.0 multiply_multiply_fusion.2
  107.5 2.0 reshape.421
  109.5 1.6 fusion.60
  111.1 1.2 multiply_subtract_fusion
  112.4 0.9 copy.53
  114.0 1.4 fusion.22
  115.4 2.6 convolution_convert_fusion.3
  118.0 5.9 %convolution_convert_fusion.1 = bf16[256,5120]{1,0:T(8,128)(2,1)} fusion(bf16[256,512]{0,1:T(8,128)(2,1)} %bitcast.187, bf16[2,512,5120]{2,1,0:T(8,128)(2,1)} %param.27), kind=kOutput, calls=%fused_computation.7 | convolution fusion | flops 1343488000 | bytes 8126464 | tf_op jit(solution)/shard_map/dot_general | solution.py:530
  123.9 40.2 %shard_map.170 = (bf16[32,5120]{1,0:T(8,128)(2,1)S(1)}, bf16[8,32,5120]{2,1,0:T(8,128)(2,1)S(1)}) custom-call(bf16[8,32,5120]{2,1,0:T(8,128)(2,1)} %bitcast.137, bf16[32,5120]{1,0:T(8,128)(2,1)S(1)} %copy-done.4, f32[32,5120]{1,0:T(8,128)S(1)} %copy-done.1, f32[1,5120]{1,0:T(1,128)S(1)} %bitcast.133, f32[1,5120]{1,0:T(1,128)S(1)} %broadcast_in_dim.462.shift_ref), custom_call_target="tpu_custom_call" | custom-call | tf_op jit(solution)/shard_map/pallas_call | solution.py:201
  164.2 5.0 %multiply_reduce_fusion = (f32[256]{0:T(256)S(1)}, f32[256,512]{1,0:T(8,128)}) fusion(bf16[256,5120]{1,0:T(8,128)(2,1)S(1)} %bitcast.136, bf16[4,5120,512]{2,1,0:T(8,128)(2,1)} %param.23), kind=kOutput, calls=%fused_computation.57 | convolution fusion | flops 1342439168 | bytes 8389632 | tf_op jit(solution)/shard_map/dot_general | solution.py:543
  169.2 4.6 %shard_map.171 = f32[1,256]{1,0:T(1,128)S(1)} custom-call(f32[1,256]{1,0:T(1,128)S(1)} %bitcast.134), custom_call_target="tpu_custom_call" | custom-call | tf_op jit(solution)/shard_map/pallas_call | solution.py:236
  173.8 1.8 convert_element_type.115
  175.6 1.0 maximum_bitcast_fusion
  178.1 0.9 broadcast_in_dim.490
  178.9 2.9 scatter_fusion
  182.3 7.9 %fusion = (f32[4,256]{1,0:T(4,128)S(1)}, f32[4,256,2048]{2,1,0:T(8,128)}) fusion(pred[256,2048]{1,0:T(8,128)(4,1)S(1)} %broadcast_compare_fusion, bf16[2048,4,128]{2,1,0:T(4,128)(2,1)} %reshape_squeeze.14, f32[256,512]{1,0:T(8,128)} %get-tuple-element.80, f32[512]{0:T(512)} %bitcast.180, f32[256]{0:T(256)S(1)} %bitcast.181), kind=kOutput, calls=%fused_computation.5 | convolution fusion | flops 543554560 | bytes 11541504 | tf_op jit(solution)/shard_map/thd,shd->hts/dot_general | solution.py:392
  190.2 5.9 %fusion.24 = bf16[4,256,128]{1,2,0:T(8,128)(2,1)S(1)} fusion(bf16[2048,4,128]{2,1,0:T(4,128)(2,1)S(1)} %copy-done.16, f32[4,256,2048]{2,1,0:T(8,128)} %get-tuple-element.82, f32[4,256]{1,0:T(4,128)S(1)} %get-tuple-element.81, pred[256,2048]{1,0:T(8,128)(4,1)S(1)} %broadcast_compare_fusion), kind=kOutput, calls=%fused_computation.37 | convolution fusion | flops 545390592 | bytes 11276288 | tf_op jit(solution)/shard_map/hts,shd->thd/dot_general | solution.py:398
  196.2 3.2 convolution_convert_fusion
  199.4 40.0 %shard_map.172 = (bf16[32,5120]{1,0:T(8,128)(2,1)S(1)}, bf16[8,32,5120]{2,1,0:T(8,128)(2,1)S(1)}) custom-call(bf16[8,32,5120]{2,1,0:T(8,128)(2,1)} %bitcast.138, bf16[32,5120]{1,0:T(8,128)(2,1)S(1)} %copy-done.7, f32[1,5120]{1,0:T(1,128)S(1)} %broadcast_in_dim.465.gate_ref, f32[32,5120]{1,0:T(8,128)S(1)} %copy-done.2, f32[32,5120]{1,0:T(8,128)S(1)} %get-tuple-element.61.shift_ref), custom_call_target="tpu_custom_call" | custom-call | tf_op jit(solution)/shard_map/pallas_call | solution.py:201
  240.0 1.6 copy-done.11
  241.6 7.9 %fusion.34.own_ref = bf16[256,1024]{1,0:T(8,128)(2,1)S(1)} fusion(bf16[256,5120]{1,0:T(8,128)(2,1)} %bitcast.135, bf16[5120,1024]{1,0:T(8,128)(2,1)} %all-gather.2.cloned.1.call-done), kind=kOutput, calls=%fused_computation.45 | convolution fusion | flops 2686713856 | bytes 13631488 | tf_op jit(solution)/shard_map/dot_general | solution.py:566
  249.5 40.7 %shard_map.173 = bf16[4,256,1024]{2,1,0:T(8,128)(2,1)S(1)} custom-call(bf16[256,1024]{1,0:T(8,128)(2,1)S(1)} %fusion.34.own_ref), custom_call_target="tpu_custom_call" | custom-call | tf_op jit(solution)/shard_map/pallas_call | solution.py:301
  290.3 3.1 convolution_convert_fusion.2
  293.4 26.7 %shard_map.174 = bf16[32,5120]{1,0:T(8,128)(2,1)S(1)} custom-call(bf16[4,8,32,1280]{3,2,1,0:T(8,128)(2,1)S(1)} %bitcast.131), custom_call_target="tpu_custom_call" | custom-call | tf_op jit(solution)/shard_map/pallas_call | solution.py:342
  320.2 1.0 add_convert_fusion
  (112 shorter events, 11.0 us)
Async XLA Ops:
  7.2 283.1 %copy-start = (bf16[1024,1280]{1,0:T(8,128)(2,1)S(1)}, bf16[1024,1280]{1,0:T(8,128)(2,1)}, u32[]{:S(2)}) copy-start(bf16[1024,1280]{1,0:T(8,128)(2,1)} %param.31) | copy-start | bytes 7864324
  7.2 234.5 %all-gather.2.cloned.1.call-start = ((), (), s32[]{:S(2)}) async-start(), calls=%async_computation | async-start | bytes 13107200 | tf_op jit(solution)/shard_map/all_gather | solution.py:442
  12.5 4.0 %copy-start.32 = (s32[1,4]{1,0:T(1,128)S(1)}, s32[1,4]{1,0:T(1,128)}, u32[]{:S(2)}) copy-start(s32[1,4]{1,0:T(1,128)} %param.18) | copy-start | bytes 52
  16.5 4.3 %copy-start.22 = (f32[4,6,5120]{2,0,1:T(4,128)S(1)}, f32[4,6,5120]{2,0,1:T(4,128)}, u32[]{:S(2)}) copy-start(f32[4,6,5120]{2,0,1:T(4,128)} %param.17) | copy-start | bytes 1474564
  16.5 5.3 %copy-start.33 = (s32[4]{0:T(128)S(1)}, s32[4]{0:T(128)}, u32[]{:S(2)}) copy-start(s32[4]{0:T(128)} %param.19) | copy-start | bytes 52
  16.5 5.4 %copy-start.12 = (s32[32]{0:T(128)S(1)}, s32[32]{0:T(128)}, u32[]{:S(2)}) copy-start(s32[32]{0:T(128)} %param.20) | copy-start | bytes 388
  21.8 38.5 %copy-start.27 = (pred[32]{0:T(512)(128)(4,1)}, pred[32]{0:T(512)(128)(4,1)S(1)}, u32[]{:S(2)}) copy-start(pred[32]{0:T(512)(128)(4,1)S(1)} %get-tuple-element.73) | copy-start | bytes 100
  21.8 38.5 %copy-start.29 = (pred[32]{0:T(512)(128)(4,1)}, pred[32]{0:T(512)(128)(4,1)S(1)}, u32[]{:S(2)}) copy-start(pred[32]{0:T(512)(128)(4,1)S(1)} %get-tuple-element.74) | copy-start | bytes 100
  22.5 3.0 copy-start.5
  24.3 39.2 %copy-start.18 = (bf16[4,5120,32]{1,2,0:T(8,128)(2,1)S(1)}, bf16[4,5120,32]{1,2,0:T(8,128)(2,1)}, u32[]{:S(2)}) copy-start(bf16[4,5120,32]{1,2,0:T(8,128)(2,1)} %param.21) | copy-start | bytes 3932164
  25.5 1.0 copy-start.3
  63.5 10.0 %copy-start.14 = (bf16[8,32,5120]{2,1,0:T(8,128)(2,1)S(1)}, bf16[8,32,5120]{2,1,0:T(8,128)(2,1)}, u32[]{:S(2)}) copy-start(bf16[8,32,5120]{2,1,0:T(8,128)(2,1)} %get-tuple-element.8) | copy-start | bytes 7864324
  78.7 4.9 %copy-start.17 = (bf16[32,1,16,512]{3,2,1,0:T(8,128)(2,1)S(1)}, bf16[32,1,16,512]{3,2,1,0:T(8,128)(2,1)}, u32[]{:S(2)}) copy-start(bf16[32,1,16,512]{3,2,1,0:T(8,128)(2,1)} %get-tuple-element.22) | copy-start | bytes 1572868
  78.7 5.0 %copy-start.21 = (bf16[32,16,256]{2,1,0:T(8,128)(2,1)S(1)}, bf16[32,16,256]{2,1,0:T(8,128)(2,1)}, u32[]{:S(2)}) copy-start(bf16[32,16,256]{2,1,0:T(8,128)(2,1)} %get-tuple-element.59) | copy-start | bytes 786436
  78.7 6.1 %copy-start.15 = (bf16[8,32,5120]{2,1,0:T(8,128)(2,1)S(1)}, bf16[8,32,5120]{2,1,0:T(8,128)(2,1)}, u32[]{:S(2)}) copy-start(bf16[8,32,5120]{2,1,0:T(8,128)(2,1)} %get-tuple-element.8) | copy-start | bytes 7864324
  84.8 9.6 %copy-start.31 = (f32[3,512]{1,0:T(4,128)S(1)}, f32[3,512]{1,0:T(4,128)}, u32[]{:S(2)}) copy-start(f32[3,512]{1,0:T(4,128)} %param.24) | copy-start | bytes 18436
  109.5 3.9 %copy-start.13 = (f32[256,4,128]{2,1,0:T(4,128)S(1)}, f32[256,4,128]{2,1,0:T(4,128)}, u32[]{:S(2)}) copy-start(f32[256,4,128]{2,1,0:T(4,128)} %reshape.421) | copy-start | bytes 1572868
  111.1 2.7 copy-start.19
  111.1 2.7 copy-start.20
  118.0 5.9 %copy-start.1 = (f32[32,5120]{1,0:T(8,128)S(1)}, f32[32,5120]{1,0:T(8,128)}, u32[]{:S(2)}) copy-start(f32[32,5120]{1,0:T(8,128)} %get-tuple-element.63.gate_ref) | copy-start | bytes 1966084
  118.0 5.9 %copy-start.4 = (bf16[32,5120]{1,0:T(8,128)(2,1)S(1)}, bf16[32,5120]{1,0:T(8,128)(2,1)}, u32[]{:S(2)}) copy-start(bf16[32,5120]{1,0:T(8,128)(2,1)} %base_ref.1) | copy-start | bytes 983044
  118.0 5.9 %copy-start.10 = (f32[5120]{0:T(1024)S(1)}, f32[5120]{0:T(1024)}, u32[]{:S(2)}) copy-start(f32[5120]{0:T(1024)} %param.28) | copy-start | bytes 61444
  164.1 5.0 %copy-start.6 = (bf16[32,5120]{1,0:T(8,128)(2,1)}, bf16[32,5120]{1,0:T(8,128)(2,1)S(1)}, u32[]{:S(2)}) copy-start(bf16[32,5120]{1,0:T(8,128)(2,1)S(1)} %get-tuple-element.11.base_ref) | copy-start | bytes 983044
  182.3 7.9 %copy-start.16 = (bf16[2048,4,128]{2,1,0:T(4,128)(2,1)S(1)}, bf16[2048,4,128]{2,1,0:T(4,128)(2,1)}, u32[]{:S(2)}) copy-start(bf16[2048,4,128]{2,1,0:T(4,128)(2,1)} %reshape.457) | copy-start | bytes 6291460
  182.3 13.8 %slice-start = ((s8[10485760]{0:T(1024)(128)(4,1)}), s8[4194304]{0:T(1024)(128)(4,1)S(1)}, s32[]{:S(2)}) async-start(s8[10485760]{0:T(1024)(128)(4,1)} %bitcast.183), calls=%async_computation.1 | async-start | bytes 8388608
  190.1 6.0 %slice-start.1 = ((s8[10485760]{0:T(1024)(128)(4,1)}), s8[4194304]{0:T(1024)(128)(4,1)S(1)}, s32[]{:S(2)}) async-start(s8[10485760]{0:T(1024)(128)(4,1)} %bitcast.183), calls=%async_computation.2 | async-start | bytes 8388608
  190.2 6.0 %slice-start.2 = ((s8[10485760]{0:T(1024)(128)(4,1)}), s8[2097152]{0:T(1024)(128)(4,1)S(1)}, s32[]{:S(2)}) async-start(s8[10485760]{0:T(1024)(128)(4,1)} %bitcast.183), calls=%async_computation.3 | async-start | bytes 4194304
  196.1 3.2 copy-start.2
  196.1 3.2 copy-start.7
  239.3 0.7 copy-start.8
  240.0 1.6 copy-start.11
  293.4 26.8 %copy-start.9 = (bf16[32,5120]{1,0:T(8,128)(2,1)S(1)}, bf16[32,5120]{1,0:T(8,128)(2,1)}, u32[]{:S(2)}) copy-start(bf16[32,5120]{1,0:T(8,128)(2,1)} %copy-done.8) | copy-start | bytes 983044
  293.4 26.8 %copy-start.23 = (f32[1,1,5120]{2,0,1:T(1,128)S(1)}, f32[1,1,5120]{2,0,1:T(1,128)}, u32[]{:S(2)}) copy-start(f32[1,1,5120]{2,0,1:T(1,128)} %get-tuple-element.28) | copy-start | bytes 61444
  293.4 26.8 %copy-start.24 = (f32[1,1,5120]{2,0,1:T(1,128)S(1)}, f32[1,1,5120]{2,0,1:T(1,128)}, u32[]{:S(2)}) copy-start(f32[1,1,5120]{2,0,1:T(1,128)} %get-tuple-element.29) | copy-start | bytes 61444
  293.4 26.8 %copy-start.25 = (f32[1,1,5120]{2,0,1:T(1,128)S(1)}, f32[1,1,5120]{2,0,1:T(1,128)}, u32[]{:S(2)}) copy-start(f32[1,1,5120]{2,0,1:T(1,128)} %get-tuple-element.47) | copy-start | bytes 61444
  293.4 26.8 %copy-start.26 = (f32[1,1,5120]{2,0,1:T(1,128)S(1)}, f32[1,1,5120]{2,0,1:T(1,128)}, u32[]{:S(2)}) copy-start(f32[1,1,5120]{2,0,1:T(1,128)} %get-tuple-element.51) | copy-start | bytes 61444
  293.4 26.8 %copy-start.28 = (pred[32]{0:T(512)(128)(4,1)S(1)}, pred[32]{0:T(512)(128)(4,1)}, u32[]{:S(2)}) copy-start(pred[32]{0:T(512)(128)(4,1)} %copy-done.27) | copy-start | bytes 100
  293.4 26.8 %copy-start.30 = (pred[32]{0:T(512)(128)(4,1)S(1)}, pred[32]{0:T(512)(128)(4,1)}, u32[]{:S(2)}) copy-start(pred[32]{0:T(512)(128)(4,1)} %copy-done.29) | copy-start | bytes 100
Sparse Core Ops, SparseCore 0:
  9.6 186.6 all-gather.1

commit v2 on v1

--- a/solution.py
+++ b/solution.py
@@ -21,7 +21,7 @@
 VM = pl.BlockSpec(memory_space=pltpu.VMEM)
 
 
-def comm_call(kernel, out_shape, in_specs, out_specs, scratch, ident):
+def comm_call(kernel, out_shape, in_specs, out_specs, scratch, ident, room=4):
     return pl.pallas_call(
         kernel,
         out_shape=out_shape,
@@ -29,7 +29,7 @@
         out_specs=out_specs,
         scratch_shapes=scratch,
         compiler_params=pltpu.CompilerParams(
-            collective_id=ident, has_side_effects=True, vmem_limit_bytes=48 << 20
+            collective_id=ident, has_side_effects=True, vmem_limit_bytes=room << 20
         ),
     )
 
@@ -141,6 +141,7 @@
         [pltpu.VMEM((rows, width), jnp.bfloat16), dma(()), dma((count - 1,)), dma((count - 1,))]
         + gather_sems(count),
         0,
+        8,
     )(tokens, scale, shift_rows, maps)
     return gathered.reshape(count * rows, width), up
 
@@ -208,6 +209,7 @@
         (VM, ANY),
         scratch[:3] + [pltpu.VMEM((rows, width), jnp.bfloat16)] + scratch[3:] + gather_sems(count),
         ident,
+        24,
     )(part.reshape(count, rows, width), base, gate, scale, shift_rows)
     return res, gathered.reshape(count * rows, width)
 
@@ -349,6 +351,7 @@
         + scratch[3:]
         + [dma(()), dma((lines - 1,)), dma((lines - 1,))],
         ident,
+        24,
     )(part)
 
 
@@ -362,7 +365,9 @@
     half_dim = HD // 2
     spatial = half_dim // 3
     temporal = half_dim - 2 * spatial
-    column = jnp.arange(half_dim, dtype=jnp.int32)
+    column = jnp.arange(HD, dtype=jnp.int32)
+    sign = jnp.where(column < half_dim, -1.0, 1.0).astype(jnp.float32)
+    column = column % half_dim
     which_axis = jnp.where(
         column < temporal, 0, jnp.where(column < temporal + spatial, 1, 2)
     ).astype(jnp.int32)
@@ -371,33 +376,117 @@
     ).astype(jnp.int32)
     span_size = jnp.where(which_axis == 0, temporal, spatial).astype(jnp.float32)
     frequency = jnp.exp(-(column - offset).astype(jnp.float32) / span_size * math.log(10000.0))
-    coordinate = grid.astype(jnp.float32)[which_axis, :].T
+    grid = grid.astype(jnp.float32)[:, :, None]
+    coordinate = jnp.where(
+        which_axis == 0, grid[0], jnp.where(which_axis == 1, grid[1], grid[2])
+    )
     angles = coordinate * frequency[None, :]
-    return (jnp.cos(angles), jnp.sin(angles))
-
-
-def rotate(values, cosine, sine_part):
-    half_dim = HD // 2
-    front_half = values[..., :half_dim]
-    back_half = values[..., half_dim:]
-    cosine = cosine[:, None, :]
-    sine_part = sine_part[:, None, :]
-    return jnp.concatenate(
-        [front_half * cosine - back_half * sine_part, back_half * cosine + front_half * sine_part],
-        axis=-1,
-    )
+    return (jnp.cos(angles), jnp.sin(angles) * sign[None, :])
 
 
 def attend(queries, key_rows, value_rows, allowed):
-    scores = jnp.einsum(
-        "thd,shd->hts", queries, key_rows, preferred_element_type=jnp.float32
-    ) / math.sqrt(HD)
-    scores = jnp.where(allowed[None], scores, -1e30)
-    weights = jnp.exp(scores)
-    weights = (weights / jnp.sum(weights, axis=-1, keepdims=True)).astype(jnp.bfloat16)
-    return jnp.einsum(
-        "hts,shd->thd", weights, value_rows, preferred_element_type=jnp.float32
+    scores = lax.dot_general(
+        queries, key_rows, (((1,), (1,)), ((), ())), preferred_element_type=jnp.float32
+    ) * (1.0 / math.sqrt(HD))
+    weights = jnp.exp(jnp.where(allowed, scores, -1e30))
+    weights = weights * (1.0 / jnp.sum(weights, axis=-1, keepdims=True))
+    return jnp.dot(
+        weights.astype(jnp.bfloat16), value_rows, preferred_element_type=jnp.float32
     ).astype(jnp.bfloat16)
+
+
+def self_kernel(page_ref, q_ref, k_ref, v_ref, qs_ref, ks_ref, gain_ref, cos_ref, sin_ref, seg_ref, segs_ref, out_ref, kv_ref):
+    cosine, sine = cos_ref[...], sin_ref[...]
+    allowed = seg_ref[...] == segs_ref[...]
+
+    def turned(ref, scale, gain, columns):
+        rows = ref[:, columns] * scale * gain_ref[gain : gain + 1, columns]
+        return (rows * cosine + pltpu.roll(rows, HD // 2, 1) * sine).astype(jnp.bfloat16)
+
+    for head in range(q_ref.shape[1] // HD):
+        columns = slice(head * HD, (head + 1) * HD)
+        query = turned(q_ref, qs_ref[...], 0, columns)
+        key = turned(k_ref, ks_ref[...], 1, columns)
+        value = v_ref[:, columns]
+        out_ref[:, columns] = attend(query, key, value, allowed)
+        for block in range(kv_ref.shape[1]):
+            page = page_ref[block]
+            rows = slice(block * PAGE, (block + 1) * PAGE)
+            kv_ref[0, page, :, columns] = key[rows]
+            kv_ref[1, page, :, columns] = value[rows]
+
+
+def self_attention(pages, query, key, value, query_scale, key_scale, gains, cosine, sine, segment):
+    rows, width = query.shape
+    return pl.pallas_call(
+        self_kernel,
+        out_shape=(
+            jax.ShapeDtypeStruct((rows, width), jnp.bfloat16),
+            jax.ShapeDtypeStruct((2, pages.shape[0], PAGE, width), jnp.bfloat16),
+        ),
+        in_specs=[pl.BlockSpec(memory_space=pltpu.SMEM)] + [VM] * 10,
+        out_specs=(VM, VM),
+        compiler_params=pltpu.CompilerParams(vmem_limit_bytes=16 << 20),
+    )(
+        pages,
+        query,
+        key,
+        value,
+        query_scale[:, None],
+        key_scale[:, None],
+        gains,
+        cosine,
+        sine,
+        segment[:, None],
+        segment[None, :],
+    )
+
+
+def cross_kernel(q_ref, k_ref, v_ref, seg_ref, owner_ref, out_ref):
+    out_ref[...] = attend(q_ref[...], k_ref[0], v_ref[0], seg_ref[...] == owner_ref[...])
+
+
+def cross_attention(query, cache, segment, owner):
+    rows, width = query.shape
+    texts = cache.shape[1]
+    head = pl.BlockSpec((rows, HD), lambda h: (0, h))
+    return pl.pallas_call(
+        cross_kernel,
+        out_shape=jax.ShapeDtypeStruct((rows, width), jnp.bfloat16),
+        grid=(width // HD,),
+        in_specs=[
+            head,
+            pl.BlockSpec((1, texts, HD), lambda h: (0, 0, h)),
+            pl.BlockSpec((1, texts, HD), lambda h: (1, 0, h)),
+            pl.BlockSpec((rows, 1), lambda h: (0, 0)),
+            pl.BlockSpec((1, texts), lambda h: (0, 0)),
+        ],
+        out_specs=head,
+        compiler_params=pltpu.CompilerParams(vmem_limit_bytes=24 << 20),
+    )(query, cache, cache, segment[:, None], owner[None, :])
+
+
+def product_kernel(act, x_ref, w_ref, out_ref):
+    out_ref[0] = act(
+        jnp.dot(x_ref[...], w_ref[0], preferred_element_type=jnp.float32)
+    ).astype(out_ref.dtype)
+
+
+def product(rows_in, maps, first, amount, tile, dtype, act=lambda part: part):
+    rows, depth = rows_in.shape
+    width = maps.shape[2]
+    tile = min(tile, width)
+    return pl.pallas_call(
+        functools.partial(product_kernel, act),
+        out_shape=jax.ShapeDtypeStruct((amount, rows, width), dtype),
+        grid=(amount, width // tile),
+        in_specs=[
+            pl.BlockSpec((rows, depth), lambda i, j: (0, 0)),
+            pl.BlockSpec((1, depth, tile), lambda i, j: (first + i, 0, j)),
+        ],
+        out_specs=pl.BlockSpec((1, rows, tile), lambda i, j: (i, 0, j)),
+        compiler_params=pltpu.CompilerParams(vmem_limit_bytes=24 << 20),
+    )(rows_in, maps)
 
 
 def choose_rows(table, segment):
@@ -431,7 +520,6 @@
     own_count = tokens.shape[0]
     group_rows = own_count * mlp_count
     local_width = input_projection.shape[2]
-    heads_local = local_width // HD
     entire_width = local_width * mlp_count
     resident_slots = adapter_down_weight.shape[0]
     doubled_rank = adapter_down_weight.shape[2]
@@ -451,7 +539,14 @@
         tokens, per_token[1], per_token[0], adapter_up_maps, mlp_count
     )
     request_slot = adapter_storage[request_adapter]
-    token_slot = choose_rows(request_slot, segment)
+    token_slot = jnp.sum(
+        jnp.where(
+            segment[:, None] == jnp.arange(request_slot.shape[0], dtype=jnp.int32)[None, :],
+            request_slot[None, :],
+            0,
+        ),
+        axis=1,
+    )
     resident = my_index * resident_slots + jnp.arange(resident_slots, dtype=jnp.int32)
     held = (token_slot[None, :] == resident[:, None]).astype(jnp.float32)
     code_block = lax.dot_general(
@@ -478,12 +573,10 @@
             preferred_element_type=jnp.float32,
         )
 
-    def project(which_map):
-        return jnp.dot(rows_in, input_projection[which_map], preferred_element_type=jnp.float32)
-
-    query_linear = project(0) + adapted(codes[:rank_once], 0)
-    key_linear = project(1)
-    value_rows = (project(2) + adapted(codes[rank_once:], 1)).astype(jnp.bfloat16)
+    projected = product(rows_in, input_projection, 0, 3, 256, jnp.float32)
+    query_linear = projected[0] + adapted(codes[:rank_once], 0)
+    key_linear = projected[1]
+    value_rows = (projected[2] + adapted(codes[rank_once:], 1)).astype(jnp.bfloat16)
     squares = small_sum(
         jnp.stack(
             [jnp.sum(query_linear * query_linear, axis=1), jnp.sum(key_linear * key_linear, axis=1)]
@@ -492,44 +585,26 @@
         2,
     )
     query_square, key_square = squares[0], squares[1]
-    query_norm = (
-        query_linear
-        * lax.rsqrt(query_square / entire_width + EPSILON)[:, None]
-        * query_key_gains[0]
-    )
-    key_norm = (
-        key_linear * lax.rsqrt(key_square / entire_width + EPSILON)[:, None] * query_key_gains[1]
-    )
-    cosine, sine_part = rotary_tables(positions)
-    query_rot = rotate(query_norm.reshape(group_rows, heads_local, HD), cosine, sine_part).astype(
-        jnp.bfloat16
-    )
-    key_rot = rotate(key_norm.reshape(group_rows, heads_local, HD), cosine, sine_part).astype(
-        jnp.bfloat16
-    )
-    value_heads = value_rows.reshape(group_rows, heads_local, HD)
-    page_count = group_rows // PAGE
-    stacked = jnp.stack(
-        [
-            key_rot.reshape(page_count, PAGE, local_width),
-            value_rows.reshape(page_count, PAGE, local_width),
-        ]
-    )
-    kv_pages = jnp.zeros_like(stacked).at[:, block_page_lookup[0]].set(stacked)
-    allowed = segment[:, None] == segment[None, :]
-    attended = attend(query_rot, key_rot, value_heads, allowed).reshape(group_rows, local_width)
+    cosine, sine = rotary_tables(positions)
+    attended, kv_pages = self_attention(
+        block_page_lookup[0],
+        query_linear,
+        key_linear,
+        value_rows,
+        lax.rsqrt(query_square / entire_width + EPSILON),
+        lax.rsqrt(key_square / entire_width + EPSILON),
+        query_key_gains,
+        cosine,
+        sine,
+        segment,
+    )
     text_owner = (
         jnp.arange(text_token_cache.shape[1] * text_token_cache.shape[2], dtype=jnp.int32)
         // text_token_cache.shape[2]
     )
-    cross_allowed = segment[:, None] == text_owner[None, :]
-    text_keys = text_token_cache[0].reshape(-1, heads_local, HD)
-    text_values = text_token_cache[1].reshape(-1, heads_local, HD)
 
     def out_rows(rows, which_map):
-        return jnp.dot(
-            rows, output_projection[which_map], preferred_element_type=jnp.float32
-        ).astype(jnp.bfloat16)
+        return product(rows, output_projection, which_map, 1, 1280, jnp.bfloat16)[0]
 
     first_res, cross_in = middle_rows(
         out_rows(attended, 0),
@@ -540,7 +615,7 @@
         mlp_count,
         3,
     )
-    cross_linear = jnp.dot(cross_in, input_projection[3], preferred_element_type=jnp.float32)
+    cross_linear = product(cross_in, input_projection, 3, 1, 256, jnp.float32)[0]
     cross_square = small_sum(
         jnp.sum(cross_linear * cross_linear, axis=1)[None, :], mlp_count, 4
     )[0]
@@ -549,10 +624,12 @@
         * lax.rsqrt(cross_square / entire_width + EPSILON)[:, None]
         * query_key_gains[2]
     ).astype(jnp.bfloat16)
-    cross_out = attend(
-        cross_query.reshape(group_rows, heads_local, HD), text_keys, text_values, cross_allowed
-    ).reshape(group_rows, local_width)
-
+    cross_out = cross_attention(
+        cross_query,
+        text_token_cache.reshape(2, text_owner.shape[0], local_width),
+        segment,
+        text_owner,
+    )
     second_res, mlp_in = middle_rows(
         out_rows(cross_out, 1),
         first_res,
@@ -562,9 +639,15 @@
         mlp_count,
         5,
     )
-    hidden = jax.nn.gelu(
-        jnp.dot(mlp_in, up_full, preferred_element_type=jnp.float32), approximate=True
-    ).astype(jnp.bfloat16)
+    hidden = product(
+        mlp_in,
+        up_full[None],
+        0,
+        1,
+        256,
+        jnp.bfloat16,
+        functools.partial(jax.nn.gelu, approximate=True),
+    )[0]
     hidden_all = line_gather(hidden, req_count, 6)
     units, columns = feedforward_down.shape
     down_part = jnp.dot(

time: 329 us -> 289 us (0.88)
  matrix products: 60.3 us -> 9.12 us
  Pallas kernels: 196 us -> 219 us
  other arithmetic: 17.2 us -> 6.19 us
    dot_general x11 -> x0, matrix products: 52.9 us -> none  [the longest x3 13.1 us: project(): jnp.dot(rows_in, input_projection[which_map], preferred_element_type=jnp....]
    unnamed x74 -> x90, local copies, waits for them, and re-layouts: 3.47 us -> 32.6 us
    pallas_call x0 -> x7, Pallas kernels: none -> 26.6 us  [the longest x5 18.4 us: product(): pl.pallas_call(functools.partial(product_kernel, act), out_shape=jax.Shap...]
    another operation x3 -> x0, local copies, waits for them, and re-layouts: 8.87 us -> none  [the longest x1 4.05 us: body(): text_keys = text_token_cache[0].reshape(-1, heads_local, HD)]
    slice x4 -> x2, local copies, waits for them, and re-layouts: 6.52 us -> 0.8 us  [the longest x1 0.8 us: rotary_tables(): grid[0]]
    reshape x3 -> x0, local copies, waits for them, and re-layouts: 4.85 us -> none  [the longest x1 2.01 us: body(): key_norm.reshape(group_rows, heads_local, HD)]
    pallas_call x2, Pallas kernels: 80.2 us -> 76.8 us  [middle_rows(): comm_call(functools.partial(middle_kernel, count), (jax.ShapeDtypeStruct(...]
  transfers between devices with their start and end apart: 1 -> 1, of which waited for: 0 -> 0; matrix products, arithmetic and copies ran while one was open for 31% -> 6% of each run, Pallas kernels for 39% -> 51%
where the time goes in v2:
time: 289 us; the launch traced here: 288 us
  Pallas kernels  219 us (76%)
  local copies, waits for them, and re-layouts  38.7 us (13%)
  between operations  14.7 us (5%)
  matrix products  9.12 us (3%)
  other arithmetic  6.19 us (2%)
    pallas_call x2, Pallas kernels, middle_rows(): comm_call(functools.partial(middle_kernel, count), (jax.ShapeDtypeStruct(...  76.8 us
    pallas_call x1, Pallas kernels, line_gather(): comm_call(functools.partial(line_kernel, count), jax.ShapeDtypeStruct((co...  40.9 us
    pallas_call x1, Pallas kernels, entry_rows(): comm_call(functools.partial(entry_kernel, count), (jax.ShapeDtypeStruct((...  33.2 us
    unnamed x90, local copies, waits for them, and re-layouts  32.6 us
    pallas_call x1, Pallas kernels, exit_rows(): comm_call(functools.partial(exit_kernel, count, lines), jax.ShapeDtypeStr...  26.8 us
    pallas_call x5, Pallas kernels, product(): pl.pallas_call(functools.partial(product_kernel, act), out_shape=jax.Shap...  18.4 us
    pallas_call x3, Pallas kernels, small_sum(): comm_call(functools.partial(small_kernel, count), jax.ShapeDtypeStruct(ow...  14.8 us
  transfers between devices with their start and end apart: 1, of which 0 were waited for; matrix products, arithmetic and copies ran while one was open for 6% of the time, Pallas kernels for 51%

profile of v2, /device:TPU:0, one launch (start us, length us, event | category | flops | bytes accessed | tf_op | source)
XLA Modules:
  0.0 288.5 jit_solution(10408675814447307141)
XLA Ops:
  7.2 0.7 all-gather.2.cloned.1.call-update
  8.0 0.2 reduce-window.8
  8.4 0.7 fusion.7
  9.1 0.9 fusion.6
  10.0 1.1 select_add_fusion
  11.1 1.2 select_select_fusion
  12.3 1.0 copy-done.14
  13.3 33.2 %shard_map.167 = (bf16[8,32,5120]{2,1,0:T(8,128)(2,1)S(1)}, bf16[32,2,16,512]{3,2,1,0:T(8,128)(2,1)S(1)}) custom-call(bf16[32,5120]{1,0:T(8,128)(2,1)S(1)} %copy-done.14, f32[32,5120]{1,0:T(8,128)S(1)} %get-tuple-element.59.scale_ref, f32[32,5120]{1,0:T(8,128)S(1)} %get-tuple-element.56.shift_ref, bf16[4,2,16,4096]{3,2,1,0:T(8,128)(2,1)S(1)} %copy-done.18), custom_call_target="tpu_custom_call" | custom-call | tf_op jit(solution)/shard_map/pallas_call | solution.py:133
  46.5 1.0 copy-done.16
  47.5 8.0 %copy-done.1 = bf16[4,5120,512]{2,1,0:T(8,128)(2,1)S(1)} copy-done((bf16[4,5120,512]{2,1,0:T(8,128)(2,1)S(1)}, bf16[4,5120,512]{2,1,0:T(8,128)(2,1)}, u32[]{:S(2)}) %copy-start.1) | copy-done | bytes 20971544
  55.5 6.2 %shard_map.168 = f32[3,256,512]{2,1,0:T(8,128)S(1)} custom-call(bf16[256,5120]{1,0:T(8,128)(2,1)S(1)} %bitcast.97, bf16[4,5120,512]{2,1,0:T(8,128)(2,1)S(1)} %copy-done.1), custom_call_target="tpu_custom_call" | custom-call | tf_op jit(solution)/shard_map/pallas_call | solution.py:479
  61.8 1.1 copy-done.7
  62.9 0.6 gather_fusion
  63.7 3.3 %fusion.10 = f32[256,128]{0,1:T(8,128)S(1)} fusion(bf16[256,5120]{1,0:T(8,128)(2,1)} %bitcast.98, bf16[128,5120]{1,0:T(8,128)(2,1)} %bitcast.112), kind=kOutput, calls=%fused_computation.61 | convolution fusion | flops 335544320 | bytes 4063232 | tf_op jit(solution)/shard_map/dot_general | solution.py:552
  67.0 5.4 %shard_map.169 = f32[32,256]{1,0:T(8,128)S(1)} custom-call(bf16[32,256]{1,0:T(8,128)(2,1)S(1)} %multiply_reduce_fusion.2.own_ref), custom_call_target="tpu_custom_call" | custom-call | tf_op jit(solution)/shard_map/pallas_call | solution.py:238
  72.5 0.1 multiply_reduce_fusion
  72.6 0.8 broadcast_select_fusion
  73.4 0.9 fusion.5
  74.2 1.2 multiply_reduce_fusion.1
  75.4 4.7 %shard_map.170 = f32[2,256]{1,0:T(2,128)S(1)} custom-call(f32[2,256]{1,0:T(2,128)S(1)} %pad_maximum_fusion.own_ref), custom_call_target="tpu_custom_call" | custom-call | tf_op jit(solution)/shard_map/pallas_call | solution.py:238
  80.1 0.1 copy.22.qs_ref
  80.3 0.8 copy.23.ks_ref
  81.1 0.6 convert_element_type.56
  81.7 0.1 copy.24.seg_ref
  81.9 0.8 fusion.9
  82.7 0.6 sine_multiply_fusion
  83.3 1.1 slice_bitcast_fusion.1.k_ref
  84.4 1.6 fusion.v_ref
  86.1 2.9 %shard_map.171 = (bf16[256,512]{1,0:T(8,128)(2,1)S(1)}, bf16[2,16,16,512]{3,2,1,0:T(8,128)(2,1)}) custom-call(s32[16]{0:T(128)S(1)} %bitcast.109, f32[256,512]{1,0:T(8,128)S(1)} %copy-done.13, f32[256,512]{1,0:T(8,128)S(1)} %slice_bitcast_fusion.1.k_ref, bf16[256,512]{1,0:T(8,128)(2,1)S(1)} %fusion.v_ref, f32[256,1]{1,0:T(8,128)S(1)} %copy.22.qs_ref, ...), custom_call_target="tpu_custom_call" | custom-call | tf_op jit(solution)/shard_map/pallas_call | solution.py:421
  89.0 4.1 %copy-done.3 = bf16[2,512,5120]{2,1,0:T(8,128)(2,1)S(1)} copy-done((bf16[2,512,5120]{2,1,0:T(8,128)(2,1)S(1)}, bf16[2,512,5120]{2,1,0:T(8,128)(2,1)}, u32[]{:S(2)}) %copy-start.3) | copy-done | bytes 10485784
  93.1 2.6 shard_map.172
  95.7 38.5 %shard_map.173 = (bf16[32,5120]{1,0:T(8,128)(2,1)S(1)}, bf16[8,32,5120]{2,1,0:T(8,128)(2,1)S(1)}) custom-call(bf16[8,32,5120]{2,1,0:T(8,128)(2,1)S(1)} %bitcast.95, bf16[32,5120]{1,0:T(8,128)(2,1)S(1)} %copy-done.15, f32[32,5120]{1,0:T(8,128)S(1)} %copy-done.9, f32[1,5120]{1,0:T(1,128)S(1)} %bitcast.105, f32[1,5120]{1,0:T(1,128)S(1)} %broadcast_in_dim.455.shift_ref), custom_call_target="tpu_custom_call" | custom-call | tf_op jit(solution)/shard_map/pallas_call | solution.py:202
  134.2 7.0 %copy-done.2 = bf16[4,5120,512]{2,1,0:T(8,128)(2,1)S(1)} copy-done((bf16[4,5120,512]{2,1,0:T(8,128)(2,1)S(1)}, bf16[4,5120,512]{2,1,0:T(8,128)(2,1)}, u32[]{:S(2)}) %copy-start.2) | copy-done | bytes 20971544
  141.2 2.1 shard_map.174
  143.4 4.7 %shard_map.175 = f32[1,256]{1,0:T(1,128)S(1)} custom-call(f32[1,256]{1,0:T(1,128)S(1)} %bitcast.108), custom_call_target="tpu_custom_call" | custom-call | tf_op jit(solution)/shard_map/pallas_call | solution.py:238
  148.3 2.2 copy-done.4
  150.4 5.2 %shard_map.176.x_ref = bf16[256,512]{1,0:T(8,128)(2,1)S(1)} custom-call(bf16[256,512]{1,0:T(8,128)(2,1)S(1)} %fusion.3.q_ref, bf16[2,2048,512]{2,1,0:T(8,128)(2,1)S(1)} %bitcast.93, bf16[2,2048,512]{2,1,0:T(8,128)(2,1)S(1)} %bitcast.94, s32[256,1]{1,0:T(8,128)S(1)} %copy.24.seg_ref, s32[1,2048]{1,0:T(1,128)S(1)} %and_select_fusion.owner_ref), custom_call_target="tpu_custom_call" | custom-call | tf_op jit(solution)/shard_map/pallas_call | solution.py:453
  155.7 2.6 shard_map.177
  158.4 38.3 %shard_map.178 = (bf16[32,5120]{1,0:T(8,128)(2,1)S(1)}, bf16[8,32,5120]{2,1,0:T(8,128)(2,1)S(1)}) custom-call(bf16[8,32,5120]{2,1,0:T(8,128)(2,1)S(1)} %bitcast.96, bf16[32,5120]{1,0:T(8,128)(2,1)S(1)} %get-tuple-element.14.base_ref, f32[1,5120]{1,0:T(1,128)S(1)} %broadcast_in_dim.457.gate_ref, f32[32,5120]{1,0:T(8,128)S(1)} %copy-done.10, ...), custom_call_target="tpu_custom_call" | custom-call | tf_op jit(solution)/shard_map/pallas_call | solution.py:202
  196.7 1.6 copy-done.11
  198.3 0.7 copy-done.20
  199.0 4.0 %copy-done.6 = bf16[5120,1024]{1,0:T(8,128)(2,1)S(1)} copy-done((bf16[5120,1024]{1,0:T(8,128)(2,1)S(1)}, bf16[5120,1024]{1,0:T(8,128)(2,1)}, u32[]{:S(2)}) %copy-start.6) | copy-done | bytes 10485784
  203.0 1.7 copy-done.12
  204.7 5.0 %shard_map.179 = bf16[1,256,1024]{2,1,0:T(8,128)(2,1)S(1)} custom-call(bf16[256,5120]{1,0:T(8,128)(2,1)S(1)} %bitcast.102, bf16[1,5120,1024]{2,1,0:T(8,128)(2,1)S(1)} %bitcast.99), custom_call_target="tpu_custom_call" | custom-call | tf_op jit(solution)/shard_map/pallas_call | solution.py:479
  209.7 40.9 %shard_map.180 = bf16[4,256,1024]{2,1,0:T(8,128)(2,1)S(1)} custom-call(bf16[256,1024]{1,0:T(8,128)(2,1)S(1)} %bitcast.104), custom_call_target="tpu_custom_call" | custom-call | tf_op jit(solution)/shard_map/pallas_call | solution.py:303
  250.6 3.1 %convolution_convert_fusion = bf16[1024,1280]{1,0:T(8,128)(2,1)S(1)} fusion(bf16[1024,1024]{1,0:T(8,128)(2,1)S(1)} %bitcast.103, bf16[1024,1280]{1,0:T(8,128)(2,1)S(1)} %copy-done), kind=kOutput, calls=%fused_computation.1 | convolution fusion | flops 2685665280 | bytes 7340032 | tf_op jit(solution)/shard_map/dot_general | solution.py:653
  253.8 26.8 %shard_map.181 = bf16[32,5120]{1,0:T(8,128)(2,1)S(1)} custom-call(bf16[4,8,32,1280]{3,2,1,0:T(8,128)(2,1)S(1)} %bitcast.101), custom_call_target="tpu_custom_call" | custom-call | tf_op jit(solution)/shard_map/pallas_call | solution.py:344
  280.6 1.0 add_convert_fusion
  (105 shorter events, 1.0 us)
Async XLA Ops:
  7.2 243.4 %copy-start = (bf16[1024,1280]{1,0:T(8,128)(2,1)S(1)}, bf16[1024,1280]{1,0:T(8,128)(2,1)}, u32[]{:S(2)}) copy-start(bf16[1024,1280]{1,0:T(8,128)(2,1)} %param.31) | copy-start | bytes 7864324
  7.2 0.8 copy-start.40
  7.2 1.2 copy-start.26
  7.2 191.8 %all-gather.2.cloned.1.call-start = ((), (), s32[]{:S(2)}) async-start(), calls=%async_computation | async-start | bytes 13107200 | tf_op jit(solution)/shard_map/all_gather | solution.py:530
  8.2 4.1 %copy-start.18 = (bf16[4,2,16,4096]{3,2,1,0:T(8,128)(2,1)S(1)}, bf16[4,2,16,4096]{3,2,1,0:T(8,128)(2,1)}, u32[]{:S(2)}) copy-start(bf16[4,2,16,4096]{3,2,1,0:T(8,128)(2,1)} %maps_ref.1) | copy-start | bytes 3145732
  8.3 3.9 %copy-start.31 = (pred[32]{0:T(512)(128)(4,1)}, pred[32]{0:T(512)(128)(4,1)S(1)}, u32[]{:S(2)}) copy-start(pred[32]{0:T(512)(128)(4,1)S(1)} %get-tuple-element.18) | copy-start | bytes 100
  8.4 3.9 %copy-start.33 = (pred[32]{0:T(512)(128)(4,1)}, pred[32]{0:T(512)(128)(4,1)S(1)}, u32[]{:S(2)}) copy-start(pred[32]{0:T(512)(128)(4,1)S(1)} %get-tuple-element.62) | copy-start | bytes 100
  8.4 3.9 %copy-start.35 = (pred[32]{0:T(512)(128)(4,1)}, pred[32]{0:T(512)(128)(4,1)S(1)}, u32[]{:S(2)}) copy-start(pred[32]{0:T(512)(128)(4,1)S(1)} %get-tuple-element.63) | copy-start | bytes 100
  8.4 3.9 %copy-start.37 = (pred[32]{0:T(512)(128)(4,1)}, pred[32]{0:T(512)(128)(4,1)S(1)}, u32[]{:S(2)}) copy-start(pred[32]{0:T(512)(128)(4,1)S(1)} %get-tuple-element.64) | copy-start | bytes 100
  12.3 1.0 copy-start.14
  46.5 1.0 copy-start.16
  47.5 14.2 %copy-start.5 = (bf16[8,32,5120]{2,1,0:T(8,128)(2,1)}, bf16[8,32,5120]{2,1,0:T(8,128)(2,1)S(1)}, u32[]{:S(2)}) copy-start(bf16[8,32,5120]{2,1,0:T(8,128)(2,1)S(1)} %get-tuple-element.10) | copy-start | bytes 7864324
  47.5 8.0 %copy-start.1 = (bf16[4,5120,512]{2,1,0:T(8,128)(2,1)S(1)}, bf16[4,5120,512]{2,1,0:T(8,128)(2,1)}, u32[]{:S(2)}) copy-start(bf16[4,5120,512]{2,1,0:T(8,128)(2,1)} %w_ref.6) | copy-start | bytes 62914564
  55.5 7.4 %copy-start.41 = (s32[4]{0:T(128)S(1)}, s32[4]{0:T(128)}, u32[]{:S(2)}) copy-start(s32[4]{0:T(128)} %param.19) | copy-start | bytes 52
  55.5 7.4 %copy-start.25 = (s32[32]{0:T(128)S(1)}, s32[32]{0:T(128)}, u32[]{:S(2)}) copy-start(s32[32]{0:T(128)} %param.20) | copy-start | bytes 388
  61.8 1.2 copy-start.7
  63.6 8.9 %copy-start.8 = (f32[3,256,512]{2,1,0:T(8,128)S(1)}, f32[3,256,512]{2,1,0:T(8,128)}, u32[]{:S(2)}) copy-start(f32[3,256,512]{2,1,0:T(8,128)} %copy-done.7) | copy-start | bytes 4718596
  63.7 9.6 %copy-start.17 = (bf16[32,2,16,512]{3,2,1,0:T(8,128)(2,1)S(1)}, bf16[32,2,16,512]{3,2,1,0:T(8,128)(2,1)}, u32[]{:S(2)}) copy-start(bf16[32,2,16,512]{3,2,1,0:T(8,128)(2,1)} %copy-done.16) | copy-start | bytes 3145732
  72.4 8.7 %copy-start.39 = (s32[3,256]{1,0:T(4,128)S(1)}, s32[3,256]{1,0:T(4,128)}, u32[]{:S(2)}) copy-start(s32[3,256]{1,0:T(4,128)} %param.25) | copy-start | bytes 9220
  72.4 9.4 %copy-start.23 = (f32[3,512]{1,0:T(4,128)S(1)}, f32[3,512]{1,0:T(4,128)}, u32[]{:S(2)}) copy-start(f32[3,512]{1,0:T(4,128)} %gain_ref.1) | copy-start | bytes 18436
  74.2 11.8 %copy-start.24 = (s32[1,16]{1,0:T(1,128)S(1)}, s32[1,16]{1,0:T(1,128)}, u32[]{:S(2)}) copy-start(s32[1,16]{1,0:T(1,128)} %param.26) | copy-start | bytes 196
  81.8 4.2 %copy-start.13 = (f32[256,512]{1,0:T(8,128)S(1)}, f32[256,512]{1,0:T(8,128)}, u32[]{:S(2)}) copy-start(f32[256,512]{1,0:T(8,128)} %get-tuple-element.66.q_ref) | copy-start | bytes 1572868
  81.9 4.2 %copy-start.19 = (f32[256,1]{1,0:T(8,128)S(1)}, f32[256,1]{1,0:T(8,128)}, u32[]{:S(2)}) copy-start(f32[256,1]{1,0:T(8,128)} %copy.23.ks_ref) | copy-start | bytes 3076
  89.0 4.1 %copy-start.3 = (bf16[2,512,5120]{2,1,0:T(8,128)(2,1)S(1)}, bf16[2,512,5120]{2,1,0:T(8,128)(2,1)}, u32[]{:S(2)}) copy-start(bf16[2,512,5120]{2,1,0:T(8,128)(2,1)} %w_ref.7) | copy-start | bytes 31457284
  93.1 2.6 copy-start.9
  93.1 2.6 copy-start.15
  93.1 2.6 copy-start.22
  93.1 62.6 %slice-start = ((s8[10485760]{0:T(1024)(128)(4,1)}), s8[4194304]{0:T(1024)(128)(4,1)S(1)}, s32[]{:S(2)}) async-start(s8[10485760]{0:T(1024)(128)(4,1)} %bitcast.91), calls=%async_computation.1 | async-start | bytes 8388608
  134.2 7.0 %copy-start.2 = (bf16[4,5120,512]{2,1,0:T(8,128)(2,1)S(1)}, bf16[4,5120,512]{2,1,0:T(8,128)(2,1)}, u32[]{:S(2)}) copy-start(bf16[4,5120,512]{2,1,0:T(8,128)(2,1)} %w_ref.6) | copy-start | bytes 62914564
  141.2 14.5 %slice-start.1 = ((s8[10485760]{0:T(1024)(128)(4,1)}), s8[4194304]{0:T(1024)(128)(4,1)S(1)}, s32[]{:S(2)}) async-start(s8[10485760]{0:T(1024)(128)(4,1)} %bitcast.91), calls=%async_computation.2 | async-start | bytes 8388608
  141.2 14.5 %slice-start.2 = ((s8[10485760]{0:T(1024)(128)(4,1)}), s8[2097152]{0:T(1024)(128)(4,1)S(1)}, s32[]{:S(2)}) async-start(s8[10485760]{0:T(1024)(128)(4,1)} %bitcast.91), calls=%async_computation.3 | async-start | bytes 4194304
  148.3 2.2 copy-start.4
  155.7 2.6 copy-start.10
  196.7 1.6 copy-start.11
  198.3 0.7 copy-start.20
  199.0 4.0 %copy-start.6 = (bf16[5120,1024]{1,0:T(8,128)(2,1)S(1)}, bf16[5120,1024]{1,0:T(8,128)(2,1)}, u32[]{:S(2)}) copy-start(bf16[5120,1024]{1,0:T(8,128)(2,1)} %all-gather.2.cloned.1.call-done) | copy-start | bytes 31457284
  203.0 1.7 copy-start.12
  253.7 26.9 %copy-start.21 = (bf16[32,5120]{1,0:T(8,128)(2,1)S(1)}, bf16[32,5120]{1,0:T(8,128)(2,1)}, u32[]{:S(2)}) copy-start(bf16[32,5120]{1,0:T(8,128)(2,1)} %copy-done.20) | copy-start | bytes 983044
  253.7 26.9 %copy-start.27 = (f32[1,1,5120]{2,0,1:T(1,128)S(1)}, f32[1,1,5120]{2,0,1:T(1,128)}, u32[]{:S(2)}) copy-start(f32[1,1,5120]{2,0,1:T(1,128)} %get-tuple-element.22) | copy-start | bytes 61444
  253.7 26.9 %copy-start.28 = (f32[1,1,5120]{2,0,1:T(1,128)S(1)}, f32[1,1,5120]{2,0,1:T(1,128)}, u32[]{:S(2)}) copy-start(f32[1,1,5120]{2,0,1:T(1,128)} %get-tuple-element.23) | copy-start | bytes 61444
  253.7 26.9 %copy-start.29 = (f32[1,1,5120]{2,0,1:T(1,128)S(1)}, f32[1,1,5120]{2,0,1:T(1,128)}, u32[]{:S(2)}) copy-start(f32[1,1,5120]{2,0,1:T(1,128)} %get-tuple-element.41) | copy-start | bytes 61444
  253.7 26.9 %copy-start.30 = (f32[1,1,5120]{2,0,1:T(1,128)S(1)}, f32[1,1,5120]{2,0,1:T(1,128)}, u32[]{:S(2)}) copy-start(f32[1,1,5120]{2,0,1:T(1,128)} %get-tuple-element.45) | copy-start | bytes 61444
  253.7 26.9 %copy-start.32 = (pred[32]{0:T(512)(128)(4,1)S(1)}, pred[32]{0:T(512)(128)(4,1)}, u32[]{:S(2)}) copy-start(pred[32]{0:T(512)(128)(4,1)} %copy-done.31) | copy-start | bytes 100
  253.7 26.9 %copy-start.34 = (pred[32]{0:T(512)(128)(4,1)S(1)}, pred[32]{0:T(512)(128)(4,1)}, u32[]{:S(2)}) copy-start(pred[32]{0:T(512)(128)(4,1)} %copy-done.33) | copy-start | bytes 100
  253.8 26.9 %copy-start.36 = (pred[32]{0:T(512)(128)(4,1)S(1)}, pred[32]{0:T(512)(128)(4,1)}, u32[]{:S(2)}) copy-start(pred[32]{0:T(512)(128)(4,1)} %copy-done.35) | copy-start | bytes 100
  253.8 26.9 %copy-start.38 = (pred[32]{0:T(512)(128)(4,1)S(1)}, pred[32]{0:T(512)(128)(4,1)}, u32[]{:S(2)}) copy-start(pred[32]{0:T(512)(128)(4,1)} %copy-done.37) | copy-start | bytes 100
Sparse Core Ops, SparseCore 0:
  9.6 186.6 all-gather.1

commit v3 on v2

--- a/solution.py
+++ b/solution.py
@@ -252,49 +252,69 @@
     own = pltpu.make_async_copy(own_ref, out_ref.at[me], own_sem)
     own.start()
 
-    def hop(step, sign):
+    pieces = rs.shape[1]
+    rows = own_ref.shape[0] // pieces
+
+    def hop(step, piece, sign):
         block = jnp.clip(me - sign * step, 0, count - 1)
-        source = own_ref if step == 0 else out_ref.at[block]
+        part = pl.ds(piece * rows, rows)
+        source = own_ref.at[part] if step == 0 else out_ref.at[block, part]
         send, recv, place = (rs, rr, right) if sign > 0 else (ls, lr, left)
-        return remote(source, out_ref.at[block], send.at[step], recv.at[step], "req", place)
-
-    for step in range(count - 1):
+        return remote(
+            source,
+            out_ref.at[block, part],
+            send.at[step, piece],
+            recv.at[step, piece],
+            "req",
+            place,
+        )
+
+    def each(step, work):
+        for piece in range(pieces):
+            work(step, piece)
+
+    def advance(step, piece):
         if step > 0:
 
             @pl.when(me >= step)
             def _():
-                hop(step - 1, 1).wait_recv()
+                hop(step - 1, piece, 1).wait_recv()
 
             @pl.when(me + step < count)
             def _():
-                hop(step - 1, -1).wait_recv()
+                hop(step - 1, piece, -1).wait_recv()
 
         @pl.when((me >= step) & (me < count - 1))
         def _():
-            hop(step, 1).start()
+            hop(step, piece, 1).start()
 
         @pl.when((me + step < count) & (me > 0))
         def _():
-            hop(step, -1).start()
-
-    @pl.when(me >= count - 1)
-    def _():
-        hop(count - 2, 1).wait_recv()
-
-    @pl.when(me < 1)
-    def _():
-        hop(count - 2, -1).wait_recv()
-
-    for step in range(count - 1):
-
+            hop(step, piece, -1).start()
+
+    def finish(step, piece):
+        @pl.when(me >= count - 1)
+        def _():
+            hop(step, piece, 1).wait_recv()
+
+        @pl.when(me < 1)
+        def _():
+            hop(step, piece, -1).wait_recv()
+
+    def drain(step, piece):
         @pl.when((me >= step) & (me < count - 1))
         def _():
-            hop(step, 1).wait_send()
+            hop(step, piece, 1).wait_send()
 
         @pl.when((me + step < count) & (me > 0))
         def _():
-            hop(step, -1).wait_send()
-
+            hop(step, piece, -1).wait_send()
+
+    for step in range(count - 1):
+        each(step, advance)
+    each(count - 2, finish)
+    for step in range(count - 1):
+        each(step, drain)
     own.wait()
 
 
@@ -305,50 +325,75 @@
         jax.ShapeDtypeStruct((count,) + own.shape, own.dtype),
         [ANY],
         ANY,
-        [dma(())] + [dma((count - 1,))] * 4,
+        [dma(())] + [dma((count - 1, 4))] * 4,
         ident,
     )(own)
 
 
 def exit_kernel(count, lines, part_ref, out_ref, near, mid, far, final, ns, nr, fs, fr, own_sem, send_sem, recv_sem):
     places = pair_places(count)
+    me, core, sibling, peers, _ = places
+    steps = count // PAIR
     line = lax.axis_index("req")
-    others = [shift(line, k, lines) for k in range(1, lines)]
+    groups = [shift(line, k + 1, lines) for k in range(lines)]
     greet(
-        [("mlp", places[2])]
-        + [("mlp", place) for place in places[3][1:]]
-        + [("req", place) for place in others]
-    )
-    final[...] = sum_blocks(
-        count, places, lambda place: part_ref.at[:, place], near, mid, far, ns, nr, fs, fr
-    ).astype(jnp.bfloat16)
+        [("mlp", sibling)]
+        + [("mlp", place) for place in peers[1:]]
+        + [("req", place) for place in groups[:-1]]
+    )
+    order = list(range(1, steps)) + [0]
+    pairs, sends, copies = {}, [], []
+    for i, group in enumerate(groups):
+        for k in order:
+            other = peers[k] + (PAIR - 1 - 2 * core)
+            pairs[i, k] = remote(
+                part_ref.at[group, other], near.at[i, k], ns.at[i, k], nr.at[i, k], "mlp", sibling
+            )
+            pairs[i, k].start()
+    for i, group in enumerate(groups):
+        for k in range(1, steps):
+            pairs[i, k].wait_recv()
+            mid[i, k] = (
+                part_ref[group, peers[k]].astype(jnp.float32) + near[i, k].astype(jnp.float32)
+            ).astype(jnp.bfloat16)
+            sends.append(
+                remote(mid.at[i, k], far.at[i, k], fs.at[i, k], fr.at[i, k], "mlp", peers[k])
+            )
+            sends[-1].start()
     width = final.shape[-1]
     target = out_ref.at[:, pl.ds(pl.multiple_of(line * width, 128), width)]
-    own = pltpu.make_async_copy(final.at[line], target, own_sem)
-    own.start()
-    copies = [
-        remote(final.at[place], target, send_sem.at[k], recv_sem.at[k], "req", place)
-        for k, place in enumerate(others)
-    ]
-    for copy in copies:
-        copy.start()
+    for i, group in enumerate(groups):
+        pairs[i, 0].wait_recv()
+        total = part_ref[group, me].astype(jnp.float32) + near[i, 0].astype(jnp.float32)
+        for k in range(1, steps):
+            sends[i * (steps - 1) + k - 1].wait_recv()
+            total = total + far[i, k].astype(jnp.float32)
+        final[i] = total.astype(jnp.bfloat16)
+        if i < lines - 1:
+            copies.append(
+                remote(final.at[i], target, send_sem.at[i], recv_sem.at[i], "req", group)
+            )
+        else:
+            copies.append(pltpu.make_async_copy(final.at[i], target, own_sem))
+        copies[-1].start()
+    for copy in list(pairs.values()) + sends:
+        copy.wait_send()
     for copy in copies:
         copy.wait()
-    own.wait()
 
 
 def exit_rows(part, count, lines, ident):
     groups, _, rows, width = part.shape
-    scratch = sum_scratch(count, (groups, rows, width))
+    steps = count // PAIR
     dma = pltpu.SemaphoreType.DMA
     return comm_call(
         functools.partial(exit_kernel, count, lines),
         jax.ShapeDtypeStruct((rows, lines * width), jnp.bfloat16),
         [VM],
         VM,
-        scratch[:3]
+        [pltpu.VMEM((groups, steps, rows, width), jnp.bfloat16)] * 3
         + [pltpu.VMEM((groups, rows, width), jnp.bfloat16)]
-        + scratch[3:]
+        + [dma((groups, steps))] * 4
         + [dma(()), dma((lines - 1,)), dma((lines - 1,))],
         ident,
         24,
@@ -486,7 +531,7 @@
         ],
         out_specs=pl.BlockSpec((1, rows, tile), lambda i, j: (i, 0, j)),
         compiler_params=pltpu.CompilerParams(vmem_limit_bytes=24 << 20),
-    )(rows_in, maps)
+    )(rows_in, pltpu.with_memory_space_constraint(maps, pltpu.HBM))
 
 
 def choose_rows(table, segment):

time: 289 us -> 272 us (0.941)
  local copies, waits for them, and re-layouts: 38.7 us -> 13.4 us
  waiting for transfers between devices: 0.68 us -> 10 us
    unnamed x90 -> x76, local copies, waits for them, and re-layouts: 32.6 us -> 7.33 us
    pallas_call x5, Pallas kernels: 18.4 us -> 29 us  [product(): pl.pallas_call(functools.partial(product_kernel, act), out_shape=jax.Shap...]
    all_gather x1, waiting for transfers between devices: 0.01 us -> 9.35 us  [body(): up_full = lax.all_gather(feedforward_up, 'req', axis=0, tiled=True)]
    pallas_call x1, Pallas kernels: 26.8 us -> 19.6 us  [exit_rows(): comm_call(functools.partial(exit_kernel, count, lines), jax.ShapeDtypeStr...]
    pallas_call x1, Pallas kernels: 40.9 us -> 36.9 us  [line_gather(): comm_call(functools.partial(line_kernel, count), jax.ShapeDtypeStruct((co...]
  transfers between devices with their start and end apart: 1 -> 1, of which waited for: 0 -> 1; matrix products, arithmetic and copies ran while one was open for 6% -> 6% of each run, Pallas kernels for 51% -> 57%
where the time goes in v3:
time: 272 us
  Pallas kernels  219 us (81%)
  between operations  14.7 us (5%)
  local copies, waits for them, and re-layouts  13.4 us (5%)
  waiting for transfers between devices  10 us (4%)
  matrix products  9.05 us (3%)
  other arithmetic  6.18 us (2%)
    pallas_call x2, Pallas kernels, middle_rows(): comm_call(functools.partial(middle_kernel, count), (jax.ShapeDtypeStruct(...  76.9 us
    pallas_call x1, Pallas kernels, line_gather(): comm_call(functools.partial(line_kernel, count), jax.ShapeDtypeStruct((co...  36.9 us
    pallas_call x1, Pallas kernels, entry_rows(): comm_call(functools.partial(entry_kernel, count), (jax.ShapeDtypeStruct((...  33.2 us
    pallas_call x5, Pallas kernels, product(): pl.pallas_call(functools.partial(product_kernel, act), out_shape=jax.Shap...  29 us
    pallas_call x1, Pallas kernels, exit_rows(): comm_call(functools.partial(exit_kernel, count, lines), jax.ShapeDtypeStr...  19.6 us
    pallas_call x3, Pallas kernels, small_sum(): comm_call(functools.partial(small_kernel, count), jax.ShapeDtypeStruct(ow...  14.8 us
    all_gather x1, waiting for transfers between devices, body(): up_full = lax.all_gather(feedforward_up, 'req', axis=0, tiled=True)  9.35 us
    unnamed x76, local copies, waits for them, and re-layouts  7.33 us
  transfers between devices with their start and end apart: 1, of which 1 were waited for; matrix products, arithmetic and copies ran while one was open for 6% of the time, Pallas kernels for 57%

profile of v3, /device:TPU:0, one launch (start us, length us, event | category | flops | bytes accessed | tf_op | source)
XLA Modules:
  0.0 272.0 jit_solution(13580443175527834150)
XLA Ops:
  7.2 0.7 all-gather.2.cloned.1.call-update
  8.0 0.2 reduce-window.8
  8.2 0.1 convert_reduce_fusion
  8.4 0.7 fusion.7
  9.1 0.9 fusion.6
  10.0 1.1 select_add_fusion
  11.1 1.2 select_select_fusion
  12.3 1.0 copy-done.10
  13.2 33.2 %shard_map.167 = (bf16[8,32,5120]{2,1,0:T(8,128)(2,1)S(1)}, bf16[32,2,16,512]{3,2,1,0:T(8,128)(2,1)S(1)}) custom-call(bf16[32,5120]{1,0:T(8,128)(2,1)S(1)} %copy-done.10, f32[32,5120]{1,0:T(8,128)S(1)} %get-tuple-element.59.scale_ref, f32[32,5120]{1,0:T(8,128)S(1)} %get-tuple-element.56.shift_ref, bf16[4,2,16,4096]{3,2,1,0:T(8,128)(2,1)S(1)} %copy-done.14), custom_call_target="tpu_custom_call" | custom-call | tf_op jit(solution)/shard_map/pallas_call | solution.py:133
  46.5 1.0 copy-done.12
  47.5 10.0 %shard_map.168 = f32[3,256,512]{2,1,0:T(8,128)S(1)} custom-call(bf16[256,5120]{1,0:T(8,128)(2,1)S(1)} %bitcast.95, bf16[4,5120,512]{2,1,0:T(8,128)(2,1)} %w_ref.6), custom_call_target="tpu_custom_call" | custom-call | tf_op jit(solution)/shard_map/pallas_call | solution.py:524
  57.6 1.1 copy-done.3
  58.7 0.6 gather_fusion
  59.4 0.1 select_reduce_fusion
  59.5 3.3 %fusion.10 = f32[256,128]{0,1:T(8,128)S(1)} fusion(bf16[256,5120]{1,0:T(8,128)(2,1)} %bitcast.96, bf16[128,5120]{1,0:T(8,128)(2,1)} %bitcast.110), kind=kOutput, calls=%fused_computation.61 | convolution fusion | flops 335544320 | bytes 4063232 | tf_op jit(solution)/shard_map/dot_general | solution.py:597
  62.8 5.4 %shard_map.169 = f32[32,256]{1,0:T(8,128)S(1)} custom-call(bf16[32,256]{1,0:T(8,128)(2,1)S(1)} %multiply_reduce_fusion.2.own_ref), custom_call_target="tpu_custom_call" | custom-call | tf_op jit(solution)/shard_map/pallas_call | solution.py:238
  68.2 0.1 multiply_reduce_fusion
  68.4 0.8 broadcast_select_fusion
  69.1 0.9 fusion.5
  70.0 1.1 multiply_reduce_fusion.1
  71.1 4.7 %shard_map.170 = f32[2,256]{1,0:T(2,128)S(1)} custom-call(f32[2,256]{1,0:T(2,128)S(1)} %pad_maximum_fusion.own_ref), custom_call_target="tpu_custom_call" | custom-call | tf_op jit(solution)/shard_map/pallas_call | solution.py:238
  75.9 0.1 copy.22.qs_ref
  76.0 0.8 copy.23.ks_ref
  76.8 0.6 convert_element_type.56
  77.4 0.1 copy.24.seg_ref
  77.6 0.8 fusion.9
  78.4 0.6 sine_multiply_fusion
  79.1 1.1 slice_bitcast_fusion.1.k_ref
  80.1 1.6 fusion.v_ref
  81.8 2.9 %shard_map.171 = (bf16[256,512]{1,0:T(8,128)(2,1)S(1)}, bf16[2,16,16,512]{3,2,1,0:T(8,128)(2,1)}) custom-call(s32[16]{0:T(128)S(1)} %bitcast.106, f32[256,512]{1,0:T(8,128)S(1)} %copy-done.9, f32[256,512]{1,0:T(8,128)S(1)} %slice_bitcast_fusion.1.k_ref, bf16[256,512]{1,0:T(8,128)(2,1)S(1)} %fusion.v_ref, f32[256,1]{1,0:T(8,128)S(1)} %copy.22.qs_ref, ...), custom_call_target="tpu_custom_call" | custom-call | tf_op jit(solution)/shard_map/pallas_call | solution.py:466
  84.7 4.5 %shard_map.172 = bf16[1,256,5120]{2,1,0:T(8,128)(2,1)S(1)} custom-call(bf16[256,512]{1,0:T(8,128)(2,1)S(1)} %get-tuple-element.12.x_ref, bf16[2,512,5120]{2,1,0:T(8,128)(2,1)} %w_ref.7), custom_call_target="tpu_custom_call" | custom-call | tf_op jit(solution)/shard_map/pallas_call | solution.py:524
  89.3 38.5 %shard_map.173 = (bf16[32,5120]{1,0:T(8,128)(2,1)S(1)}, bf16[8,32,5120]{2,1,0:T(8,128)(2,1)S(1)}) custom-call(bf16[8,32,5120]{2,1,0:T(8,128)(2,1)S(1)} %bitcast.93, bf16[32,5120]{1,0:T(8,128)(2,1)S(1)} %copy-done.11, f32[32,5120]{1,0:T(8,128)S(1)} %copy-done.5, f32[1,5120]{1,0:T(1,128)S(1)} %bitcast.102, f32[1,5120]{1,0:T(1,128)S(1)} %broadcast_in_dim.455.shift_ref), custom_call_target="tpu_custom_call" | custom-call | tf_op jit(solution)/shard_map/pallas_call | solution.py:202
  127.8 3.7 %shard_map.174 = f32[1,256,512]{2,1,0:T(8,128)S(1)} custom-call(bf16[256,5120]{1,0:T(8,128)(2,1)S(1)} %bitcast.97, bf16[4,5120,512]{2,1,0:T(8,128)(2,1)} %w_ref.6), custom_call_target="tpu_custom_call" | custom-call | tf_op jit(solution)/shard_map/pallas_call | solution.py:524
  131.5 0.1 fusion.1
  131.6 4.7 %shard_map.175 = f32[1,256]{1,0:T(1,128)S(1)} custom-call(f32[1,256]{1,0:T(1,128)S(1)} %bitcast.105), custom_call_target="tpu_custom_call" | custom-call | tf_op jit(solution)/shard_map/pallas_call | solution.py:238
  136.3 0.1 fusion.3.q_ref
  136.4 5.3 %shard_map.176.x_ref = bf16[256,512]{1,0:T(8,128)(2,1)S(1)} custom-call(bf16[256,512]{1,0:T(8,128)(2,1)S(1)} %fusion.3.q_ref, bf16[2,2048,512]{2,1,0:T(8,128)(2,1)S(1)} %bitcast.91, bf16[2,2048,512]{2,1,0:T(8,128)(2,1)S(1)} %bitcast.92, s32[256,1]{1,0:T(8,128)S(1)} %copy.24.seg_ref, s32[1,2048]{1,0:T(1,128)S(1)} %and_select_fusion.owner_ref), custom_call_target="tpu_custom_call" | custom-call | tf_op jit(solution)/shard_map/pallas_call | solution.py:498
  141.7 4.5 %shard_map.177 = bf16[1,256,5120]{2,1,0:T(8,128)(2,1)S(1)} custom-call(bf16[256,512]{1,0:T(8,128)(2,1)S(1)} %shard_map.176.x_ref, bf16[2,512,5120]{2,1,0:T(8,128)(2,1)} %w_ref.7), custom_call_target="tpu_custom_call" | custom-call | tf_op jit(solution)/shard_map/pallas_call | solution.py:524
  146.2 38.4 %shard_map.178 = (bf16[32,5120]{1,0:T(8,128)(2,1)S(1)}, bf16[8,32,5120]{2,1,0:T(8,128)(2,1)S(1)}) custom-call(bf16[8,32,5120]{2,1,0:T(8,128)(2,1)S(1)} %bitcast.94, bf16[32,5120]{1,0:T(8,128)(2,1)S(1)} %get-tuple-element.14.base_ref, f32[1,5120]{1,0:T(1,128)S(1)} %broadcast_in_dim.457.gate_ref, f32[32,5120]{1,0:T(8,128)S(1)} %copy-done.6, ...), custom_call_target="tpu_custom_call" | custom-call | tf_op jit(solution)/shard_map/pallas_call | solution.py:202
  184.6 1.6 copy-done.7
  186.2 0.7 copy-done.16
  186.9 9.4 %all-gather.2.cloned.1.call-done = bf16[5120,1024]{1,0:T(8,128)(2,1)} async-done(((bf16[1280,1024]{1,0:T(8,128)(2,1)}), bf16[5120,1024]{1,0:T(8,128)(2,1)}) %all-gather.2.cloned.1.call-update) | async-done | bytes 10485776 | tf_op jit(solution)/shard_map/all_gather | solution.py:575
  196.3 1.7 copy-done.8
  198.0 6.4 %shard_map.179 = bf16[1,256,1024]{2,1,0:T(8,128)(2,1)S(1)} custom-call(bf16[256,5120]{1,0:T(8,128)(2,1)S(1)} %bitcast.99, bf16[1,5120,1024]{2,1,0:T(8,128)(2,1)} %bitcast.107), custom_call_target="tpu_custom_call" | custom-call | tf_op jit(solution)/shard_map/pallas_call | solution.py:524
  204.4 36.9 %shard_map.180 = bf16[4,256,1024]{2,1,0:T(8,128)(2,1)S(1)} custom-call(bf16[256,1024]{1,0:T(8,128)(2,1)S(1)} %bitcast.101), custom_call_target="tpu_custom_call" | custom-call | tf_op jit(solution)/shard_map/pallas_call | solution.py:323
  241.2 3.1 %convolution_convert_fusion = bf16[1024,1280]{1,0:T(8,128)(2,1)S(1)} fusion(bf16[1024,1024]{1,0:T(8,128)(2,1)S(1)} %bitcast.100, bf16[1024,1280]{1,0:T(8,128)(2,1)S(1)} %copy-done), kind=kOutput, calls=%fused_computation.1 | convolution fusion | flops 2685665280 | bytes 7340032 | tf_op jit(solution)/shard_map/dot_general | solution.py:698
  244.4 19.6 %shard_map.181 = bf16[32,5120]{1,0:T(8,128)(2,1)S(1)} custom-call(bf16[4,8,32,1280]{3,2,1,0:T(8,128)(2,1)S(1)} %bitcast.98), custom_call_target="tpu_custom_call" | custom-call | tf_op jit(solution)/shard_map/pallas_call | solution.py:389
  264.1 1.0 add_convert_fusion
  (90 shorter events, 0.6 us)
Async XLA Ops:
  7.2 234.1 %copy-start = (bf16[1024,1280]{1,0:T(8,128)(2,1)S(1)}, bf16[1024,1280]{1,0:T(8,128)(2,1)}, u32[]{:S(2)}) copy-start(bf16[1024,1280]{1,0:T(8,128)(2,1)} %param.31) | copy-start | bytes 7864324
  7.2 0.8 copy-start.36
  7.2 1.2 copy-start.22
  7.2 189.1 %all-gather.2.cloned.1.call-start = ((), (), s32[]{:S(2)}) async-start(), calls=%async_computation | async-start | bytes 13107200 | tf_op jit(solution)/shard_map/all_gather | solution.py:575
  8.2 4.1 %copy-start.14 = (bf16[4,2,16,4096]{3,2,1,0:T(8,128)(2,1)S(1)}, bf16[4,2,16,4096]{3,2,1,0:T(8,128)(2,1)}, u32[]{:S(2)}) copy-start(bf16[4,2,16,4096]{3,2,1,0:T(8,128)(2,1)} %maps_ref.1) | copy-start | bytes 3145732
  8.3 3.9 %copy-start.27 = (pred[32]{0:T(512)(128)(4,1)}, pred[32]{0:T(512)(128)(4,1)S(1)}, u32[]{:S(2)}) copy-start(pred[32]{0:T(512)(128)(4,1)S(1)} %get-tuple-element.18) | copy-start | bytes 100
  8.4 3.9 %copy-start.29 = (pred[32]{0:T(512)(128)(4,1)}, pred[32]{0:T(512)(128)(4,1)S(1)}, u32[]{:S(2)}) copy-start(pred[32]{0:T(512)(128)(4,1)S(1)} %get-tuple-element.62) | copy-start | bytes 100
  8.4 3.9 %copy-start.31 = (pred[32]{0:T(512)(128)(4,1)}, pred[32]{0:T(512)(128)(4,1)S(1)}, u32[]{:S(2)}) copy-start(pred[32]{0:T(512)(128)(4,1)S(1)} %get-tuple-element.63) | copy-start | bytes 100
  8.4 3.9 %copy-start.33 = (pred[32]{0:T(512)(128)(4,1)}, pred[32]{0:T(512)(128)(4,1)S(1)}, u32[]{:S(2)}) copy-start(pred[32]{0:T(512)(128)(4,1)S(1)} %get-tuple-element.64) | copy-start | bytes 100
  12.3 1.0 copy-start.10
  46.5 1.0 copy-start.12
  47.5 10.1 %copy-start.2 = (bf16[8,32,5120]{2,1,0:T(8,128)(2,1)}, bf16[8,32,5120]{2,1,0:T(8,128)(2,1)S(1)}, u32[]{:S(2)}) copy-start(bf16[8,32,5120]{2,1,0:T(8,128)(2,1)S(1)} %get-tuple-element.10) | copy-start | bytes 7864324
  47.5 11.2 %copy-start.37 = (s32[4]{0:T(128)S(1)}, s32[4]{0:T(128)}, u32[]{:S(2)}) copy-start(s32[4]{0:T(128)} %param.19) | copy-start | bytes 52
  47.5 11.2 %copy-start.21 = (s32[32]{0:T(128)S(1)}, s32[32]{0:T(128)}, u32[]{:S(2)}) copy-start(s32[32]{0:T(128)} %param.20) | copy-start | bytes 388
  57.5 1.1 copy-start.3
  59.4 8.8 %copy-start.4 = (f32[3,256,512]{2,1,0:T(8,128)S(1)}, f32[3,256,512]{2,1,0:T(8,128)}, u32[]{:S(2)}) copy-start(f32[3,256,512]{2,1,0:T(8,128)} %copy-done.3) | copy-start | bytes 4718596
  59.5 9.6 %copy-start.13 = (bf16[32,2,16,512]{3,2,1,0:T(8,128)(2,1)S(1)}, bf16[32,2,16,512]{3,2,1,0:T(8,128)(2,1)}, u32[]{:S(2)}) copy-start(bf16[32,2,16,512]{3,2,1,0:T(8,128)(2,1)} %copy-done.12) | copy-start | bytes 3145732
  68.2 8.6 %copy-start.35 = (s32[3,256]{1,0:T(4,128)S(1)}, s32[3,256]{1,0:T(4,128)}, u32[]{:S(2)}) copy-start(s32[3,256]{1,0:T(4,128)} %param.25) | copy-start | bytes 9220
  68.2 9.4 %copy-start.19 = (f32[3,512]{1,0:T(4,128)S(1)}, f32[3,512]{1,0:T(4,128)}, u32[]{:S(2)}) copy-start(f32[3,512]{1,0:T(4,128)} %gain_ref.1) | copy-start | bytes 18436
  70.0 11.7 %copy-start.20 = (s32[1,16]{1,0:T(1,128)S(1)}, s32[1,16]{1,0:T(1,128)}, u32[]{:S(2)}) copy-start(s32[1,16]{1,0:T(1,128)} %param.26) | copy-start | bytes 196
  77.6 4.2 %copy-start.9 = (f32[256,512]{1,0:T(8,128)S(1)}, f32[256,512]{1,0:T(8,128)}, u32[]{:S(2)}) copy-start(f32[256,512]{1,0:T(8,128)} %get-tuple-element.66.q_ref) | copy-start | bytes 1572868
  77.6 4.2 %copy-start.15 = (f32[256,1]{1,0:T(8,128)S(1)}, f32[256,1]{1,0:T(8,128)}, u32[]{:S(2)}) copy-start(f32[256,1]{1,0:T(8,128)} %copy.23.ks_ref) | copy-start | bytes 3076
  84.7 4.5 %copy-start.5 = (f32[32,5120]{1,0:T(8,128)S(1)}, f32[32,5120]{1,0:T(8,128)}, u32[]{:S(2)}) copy-start(f32[32,5120]{1,0:T(8,128)} %get-tuple-element.57.gate_ref) | copy-start | bytes 1966084
  84.7 4.5 %copy-start.11 = (bf16[32,5120]{1,0:T(8,128)(2,1)S(1)}, bf16[32,5120]{1,0:T(8,128)(2,1)}, u32[]{:S(2)}) copy-start(bf16[32,5120]{1,0:T(8,128)(2,1)} %base_ref.1) | copy-start | bytes 983044
  84.7 4.5 %copy-start.18 = (f32[5120]{0:T(1024)S(1)}, f32[5120]{0:T(1024)}, u32[]{:S(2)}) copy-start(f32[5120]{0:T(1024)} %param.28) | copy-start | bytes 61444
  127.8 8.6 %copy-start.1 = (bf16[2,4,512,512]{3,2,1,0:T(8,128)(2,1)S(1)}, bf16[2,4,512,512]{3,2,1,0:T(8,128)(2,1)}, u32[]{:S(2)}) copy-start(bf16[2,4,512,512]{3,2,1,0:T(8,128)(2,1)} %param.29) | copy-start | bytes 12582916
  141.7 4.5 %copy-start.6 = (f32[32,5120]{1,0:T(8,128)S(1)}, f32[32,5120]{1,0:T(8,128)}, u32[]{:S(2)}) copy-start(f32[32,5120]{1,0:T(8,128)} %get-tuple-element.58.scale_ref) | copy-start | bytes 1966084
  184.6 1.6 copy-start.7
  186.2 0.7 copy-start.16
  196.3 1.7 copy-start.8
  244.3 19.7 %copy-start.17 = (bf16[32,5120]{1,0:T(8,128)(2,1)S(1)}, bf16[32,5120]{1,0:T(8,128)(2,1)}, u32[]{:S(2)}) copy-start(bf16[32,5120]{1,0:T(8,128)(2,1)} %copy-done.16) | copy-start | bytes 983044
  244.3 19.7 %copy-start.23 = (f32[1,1,5120]{2,0,1:T(1,128)S(1)}, f32[1,1,5120]{2,0,1:T(1,128)}, u32[]{:S(2)}) copy-start(f32[1,1,5120]{2,0,1:T(1,128)} %get-tuple-element.22) | copy-start | bytes 61444
  244.4 19.7 %copy-start.24 = (f32[1,1,5120]{2,0,1:T(1,128)S(1)}, f32[1,1,5120]{2,0,1:T(1,128)}, u32[]{:S(2)}) copy-start(f32[1,1,5120]{2,0,1:T(1,128)} %get-tuple-element.23) | copy-start | bytes 61444
  244.4 19.7 %copy-start.25 = (f32[1,1,5120]{2,0,1:T(1,128)S(1)}, f32[1,1,5120]{2,0,1:T(1,128)}, u32[]{:S(2)}) copy-start(f32[1,1,5120]{2,0,1:T(1,128)} %get-tuple-element.41) | copy-start | bytes 61444
  244.4 19.7 %copy-start.26 = (f32[1,1,5120]{2,0,1:T(1,128)S(1)}, f32[1,1,5120]{2,0,1:T(1,128)}, u32[]{:S(2)}) copy-start(f32[1,1,5120]{2,0,1:T(1,128)} %get-tuple-element.45) | copy-start | bytes 61444
  244.4 19.7 %copy-start.28 = (pred[32]{0:T(512)(128)(4,1)S(1)}, pred[32]{0:T(512)(128)(4,1)}, u32[]{:S(2)}) copy-start(pred[32]{0:T(512)(128)(4,1)} %copy-done.27) | copy-start | bytes 100
  244.4 19.7 %copy-start.30 = (pred[32]{0:T(512)(128)(4,1)S(1)}, pred[32]{0:T(512)(128)(4,1)}, u32[]{:S(2)}) copy-start(pred[32]{0:T(512)(128)(4,1)} %copy-done.29) | copy-start | bytes 100
  244.4 19.7 %copy-start.32 = (pred[32]{0:T(512)(128)(4,1)S(1)}, pred[32]{0:T(512)(128)(4,1)}, u32[]{:S(2)}) copy-start(pred[32]{0:T(512)(128)(4,1)} %copy-done.31) | copy-start | bytes 100
  244.4 19.7 %copy-start.34 = (pred[32]{0:T(512)(128)(4,1)S(1)}, pred[32]{0:T(512)(128)(4,1)}, u32[]{:S(2)}) copy-start(pred[32]{0:T(512)(128)(4,1)} %copy-done.33) | copy-start | bytes 100
Sparse Core Ops, SparseCore 0:
  9.6 186.6 all-gather.1
